TPU v7x, 128 devices: a whole 4x4x4 slice. The times are simulated.
128 devices in a mesh: ctx: 16 (over x_lo, z, core), head: 8 (over x_hi, y).
Axes of the slice: x: 4 (x_hi: 2, x_lo: 2; x = x_hi * 2 + x_lo), y: 4, z: 4, core: 2. Of those that a mesh axis runs over, the one named last changes fastest.
Arguments:
- queries: bfloat16 [4096, 4096], P(('ctx', 'head')), may hold values from -10 to 10
- keys: bfloat16 [4096, 4096], P(('ctx', 'head')), may hold values from -10 to 10
- values: bfloat16 [4096, 4096], P(('ctx', 'head')), may hold values from -6 to 6
- grad_out: bfloat16 [4096, 4096], P(('ctx', 'head')), may hold values from -6 to 6
- block_doc: int32 [32], replicated, may hold values from 0 to 7, as said below
Outputs:
- attn_out: bfloat16 [4096, 4096], P(('ctx', 'head'))
- d_q: bfloat16 [4096, 4096], P(('ctx', 'head'))
- d_k: bfloat16 [4096, 4096], P(('ctx', 'head'))
- d_v: bfloat16 [4096, 4096], P(('ctx', 'head'))
Inputs may be any that keep to these rules, and one draw needn't show every extreme that they name: `block_doc`: document numbers never fall; every document covers at least one block; the last document covers exactly 16 blocks and every other one fewer.
All inputs are finite; a program needn't handle non-finite values.
Results may differ from a plain program's by a relative error of at most 0.03.
Values may be sent and summed in bfloat16 or wider, within the bound.
No kernel may reach another device: no remote copies, remote signals or barrier semaphores. Data moves between devices by JAX's collectives and lax.ppermute only.
A program may use at most 128 MiB of HBM per device.

v0:
```python
import math

import jax
import jax.numpy as jnp
from jax import lax
from jax.sharding import PartitionSpec as P

HD = 128
BLK = 128


masked_low = -1e30


def document_of(block_doc, positions):
    hits = positions[:, None] // BLK == lax.iota(jnp.int32, block_doc.shape[0])[None, :]
    return jnp.sum(jnp.where(hits, block_doc[None, :], 0), axis=1)


def token_positions(first_row, count, row_count, cycle_size):
    rows = first_row + lax.iota(jnp.int32, count)
    owner = rows // row_count
    local = rows % row_count
    half = row_count // 2
    return jnp.where(
        local < half, owner * half + local, (2 * cycle_size - 1 - owner) * half + local - half
    )


def visible(block_doc, query_pos, key_pos):
    same_doc = (
        document_of(block_doc, query_pos)[:, None] == document_of(block_doc, key_pos)[None, :]
    )
    return same_doc & (key_pos[None, :] <= query_pos[:, None])


def forward_update(running, query_heads, key_part, value_part, live, score_scale):
    accum, run_max, run_sum = running
    scores = (
        jnp.einsum("qhd,khd->hqk", query_heads, key_part, preferred_element_type=jnp.float32)
        * score_scale
    )
    scores = jnp.where(live[None], scores, masked_low)
    new_max = jnp.maximum(run_max, jnp.max(scores, axis=2))
    shifted = jnp.where(live[None], jnp.exp(scores - new_max[:, :, None]), 0.0)
    fading = jnp.exp(run_max - new_max)
    new_sum = run_sum * fading + jnp.sum(shifted, axis=2)
    product = jnp.einsum(
        "hqk,khd->qhd", shifted.astype(jnp.bfloat16), value_part, preferred_element_type=jnp.float32
    )
    return (accum * fading.T[:, :, None] + product, new_max, new_sum)


def backward_tile(saved, key_part, value_part, live, score_scale):
    query_heads, grad_heads, log_total, delta = saved
    scores = (
        jnp.einsum("qhd,khd->hqk", query_heads, key_part, preferred_element_type=jnp.float32)
        * score_scale
    )
    probs = jnp.where(live[None], jnp.exp(scores - log_total[:, :, None]), 0.0)
    back_weights = probs.astype(jnp.bfloat16)
    grad_value = jnp.einsum(
        "hqk,qhd->khd", back_weights, grad_heads, preferred_element_type=jnp.float32
    )
    grad_weights = jnp.einsum(
        "qhd,khd->hqk", grad_heads, value_part, preferred_element_type=jnp.float32
    )
    grad_scores = (probs * (grad_weights - delta[:, :, None])).astype(jnp.bfloat16)
    grad_query = (
        jnp.einsum("hqk,khd->qhd", grad_scores, key_part, preferred_element_type=jnp.float32)
        * score_scale
    )
    grad_key = (
        jnp.einsum("hqk,qhd->khd", grad_scores, query_heads, preferred_element_type=jnp.float32)
        * score_scale
    )
    return (grad_query, grad_key, grad_value)


def per_device(queries, keys, values, grad_out, block_doc):
    query_here, key_here, value_here, grad_here = (
        lax.all_to_all(queries, "head", split_axis=1, concat_axis=0, tiled=True),
        lax.all_to_all(keys, "head", split_axis=1, concat_axis=0, tiled=True),
        lax.all_to_all(values, "head", split_axis=1, concat_axis=0, tiled=True),
        lax.all_to_all(grad_out, "head", split_axis=1, concat_axis=0, tiled=True),
    )
    row_count = query_here.shape[0]
    feature_width = query_here.shape[1]
    local_heads = feature_width // HD
    score_scale = HD ** (-0.5)
    cycle_size = lax.axis_size("ctx")
    position = lax.axis_index("ctx")
    query_pos = token_positions(position * row_count, row_count, row_count, cycle_size)
    query_heads = query_here.reshape(row_count, local_heads, HD)
    grad_heads = grad_here.reshape(row_count, local_heads, HD)

    def fold_keys(running, pieces, first_row):
        key_part = pieces[0].reshape(-1, local_heads, HD)
        value_part = pieces[1].reshape(-1, local_heads, HD)
        key_pos = token_positions(first_row, key_part.shape[0], row_count, cycle_size)
        live = visible(block_doc, query_pos, key_pos)
        return forward_update(running, query_heads, key_part, value_part, live, score_scale)

    start_fold = (
        jnp.zeros((row_count, local_heads, HD), jnp.float32),
        jnp.full((local_heads, row_count), masked_low, jnp.float32),
        jnp.zeros((local_heads, row_count), jnp.float32),
    )
    gathered = lax.all_gather(jnp.stack((key_here, value_here)), "ctx", axis=1, tiled=True)
    span = row_count * math.gcd(cycle_size, max(1, 512 // row_count))
    block_total = cycle_size * row_count // span

    def forward_block(block_index, running):
        first_row = block_index * span
        part = lax.dynamic_slice_in_dim(gathered, first_row, span, 1)
        return fold_keys(running, (part[0], part[1]), first_row)

    accum, run_max, run_sum = lax.fori_loop(0, block_total, forward_block, start_fold)
    out_heads = (accum / run_sum.T[:, :, None]).astype(jnp.bfloat16)
    log_total = run_max + jnp.log(run_sum)
    delta = jnp.sum(grad_heads.astype(jnp.float32) * out_heads.astype(jnp.float32), axis=2).T
    saved = (query_heads, grad_heads, log_total, delta)

    def tile_grads(key_flat, value_flat, key_start):
        key_part = key_flat.reshape(-1, local_heads, HD)
        value_part = value_flat.reshape(-1, local_heads, HD)
        key_pos = token_positions(key_start, key_part.shape[0], row_count, cycle_size)
        live = visible(block_doc, query_pos, key_pos)
        return backward_tile(saved, key_part, value_part, live, score_scale)

    def backward_block(block_index, state):
        grad_query, key_sums = state
        first_row = block_index * span
        part = lax.dynamic_slice_in_dim(gathered, first_row, span, 1)
        add_query, add_key, add_value = tile_grads(part[0], part[1], first_row)
        key_sums = lax.dynamic_update_slice_in_dim(
            key_sums, jnp.stack((add_key, add_value)), first_row, 1
        )
        return (grad_query + add_query, key_sums)

    start_back = (
        jnp.zeros((row_count, local_heads, HD), jnp.float32),
        jnp.zeros((2, cycle_size * row_count, local_heads, HD), jnp.float32),
    )
    grad_query, key_sums = lax.fori_loop(0, block_total, backward_block, start_back)
    grad_key, grad_value = (
        lax.psum_scatter(
            key_sums[0].astype(jnp.bfloat16), "ctx", scatter_dimension=0, tiled=True
        ).astype(jnp.float32),
        lax.psum_scatter(
            key_sums[1].astype(jnp.bfloat16), "ctx", scatter_dimension=0, tiled=True
        ).astype(jnp.float32),
    )
    out_flat = out_heads.reshape(row_count, feature_width)
    query_flat = grad_query.astype(jnp.bfloat16).reshape(row_count, feature_width)
    key_flat = grad_key.astype(jnp.bfloat16).reshape(row_count, feature_width)
    value_flat = grad_value.astype(jnp.bfloat16).reshape(row_count, feature_width)
    return (
        lax.all_to_all(out_flat, "head", split_axis=0, concat_axis=1, tiled=True),
        lax.all_to_all(query_flat, "head", split_axis=0, concat_axis=1, tiled=True),
        lax.all_to_all(key_flat, "head", split_axis=0, concat_axis=1, tiled=True),
        lax.all_to_all(value_flat, "head", split_axis=0, concat_axis=1, tiled=True),
    )


def solution(mesh):
    return jax.shard_map(
        per_device,
        mesh=mesh,
        in_specs=(
            P(("ctx", "head"), None),
            P(("ctx", "head"), None),
            P(("ctx", "head"), None),
            P(("ctx", "head"), None),
            P(),
        ),
        out_specs=(
            P(("ctx", "head"), None),
            P(("ctx", "head"), None),
            P(("ctx", "head"), None),
            P(("ctx", "head"), None),
        ),
        check_vma=False,
    )
```

profile of v0, /device:TPU:0, one launch (start us, length us, event | category | flops | bytes accessed | tf_op | source)
XLA Modules:
  0.0 350.0 jit_solution(4947090339236871843)
XLA Ops:
  7.2 1.7 copy.146
  8.9 7.2 %all-to-all-start = ((bf16[32,8,512]{2,0,1:T(8,128)(2,1)}), bf16[32,8,512]{2,0,1:T(8,128)(2,1)S(1)}, u32[]{:S(2)}, u32[]{:S(2)}) async-start(bf16[32,8,512]{2,0,1:T(8,128)(2,1)} %bitcast.94), calls=%async_computation | async-start | bytes 524288 | tf_op jit(solution)/shard_map/all_to_all | solution.py:83
  17.1 7.7 %all-to-all-done = bf16[32,8,512]{2,0,1:T(8,128)(2,1)S(1)} async-done(((bf16[32,8,512]{2,0,1:T(8,128)(2,1)}), bf16[32,8,512]{2,0,1:T(8,128)(2,1)S(1)}, u32[]{:S(2)}, u32[]{:S(2)}) %all-to-all-start) | async-done | bytes 262176 | tf_op jit(solution)/shard_map/all_to_all | solution.py:83
  24.8 11.3 %all_to_all.140 = bf16[32,8,512]{2,0,1:T(8,128)(2,1)S(1)} all-to-all(bf16[32,8,512]{2,0,1:T(8,128)(2,1)S(1)} %bitcast.162), channel_id=1, replica_groups=mesh['ctx'=16,'head'=8] {'head'}, dimensions={1} | all-to-all | bytes 524288 | tf_op jit(solution)/shard_map/all_to_all | solution.py:84
  37.7 3.4 all-to-all-start.2
  41.9 7.9 %all-to-all-done.2 = bf16[32,8,512]{2,0,1:T(8,128)(2,1)S(1)} async-done(((bf16[32,8,512]{2,0,1:T(8,128)(2,1)}), bf16[32,8,512]{2,0,1:T(8,128)(2,1)S(1)}, u32[]{:S(2)}, u32[]{:S(2)}) %all-to-all-start.2) | async-done | bytes 262176 | tf_op jit(solution)/shard_map/all_to_all | solution.py:82
  49.8 3.4 all-to-all-start.4
  53.4 10.4 %all-to-all-done.4 = bf16[32,8,512]{2,0,1:T(8,128)(2,1)S(1)} async-done(((bf16[32,8,512]{2,0,1:T(8,128)(2,1)}), bf16[32,8,512]{2,0,1:T(8,128)(2,1)S(1)}, u32[]{:S(2)}, u32[]{:S(2)}) %all-to-all-start.4) | async-done | bytes 262176 | tf_op jit(solution)/shard_map/all_to_all | solution.py:85
  63.9 26.2 %all-gather.2.cloned.1.call-done = bf16[2,4096,512]{2,1,0:T(8,128)(2,1)} async-done(((bf16[2,256,512]{2,1,0:T(8,128)(2,1)}), bf16[2,4096,512]{2,1,0:T(8,128)(2,1)}) %all-gather.2.cloned.1.call-update) | async-done | bytes 8388624 | tf_op jit(solution)/shard_map/all_gather | solution.py:109
  90.1 11.3 %copy.110 = bf16[2,4096,512]{1,2,0:T(8,128)(2,1)} copy(bf16[2,4096,512]{2,1,0:T(8,128)(2,1)} %all-gather.2.cloned.1.call-done) | data formatting | bytes 16777216
  101.5 29.7 %while.44 = (s32[]{:T(128)}, f32[256,4,128]{0,2,1:T(8,128)S(1)}, f32[4,256]{1,0:T(4,128)S(1)}, f32[4,256]{1,0:T(4,128)S(1)}, s32[32]{0:T(128)S(1)}, /*index=5*/b...) while((s32[]{:T(128)}, f32[256,4,128]{0,2,1:T(8,128)S(1)}, ...), condition=%wide.region_5.6_spmd.clone.clone.clone, body=%wide.region_0.5_spmd.clone.clone.clone.sunk | while | flops 276164096 | bytes 11359203 | solution.py:118
  102.0 1.3 constant_dynamic-slice_fusion.6
  105.7 1.3 constant_dynamic-slice_fusion.6
  132.3 4.3 %broadcast_in_dim.271 = bf16[2,4096,4,128]{3,1,2,0:T(8,128)(2,1)} broadcast(bf16[]{:T(256)} %constant.563), dimensions={} | broadcast | bytes 8388610 | tf_op jit(solution)/shard_map/broadcast_in_dim | solution.py:143
  136.6 43.1 %while.45 = (s32[]{:T(128)}, f32[256,4,128]{0,2,1:T(8,128)S(1)}, bf16[2,4096,4,128]{3,1,2,0:T(8,128)(2,1)}, bf16[2,4096,512]{1,2,0:T(8,128)(2,1)}, s32[32]{0:T(1...) while((s32[]{:T(128)}, f32[256,4,128]{0,2,1:T(8,128)S(1)}, ...), condition=%wide.region_10.11_spmd.clone.clone.clone, body=%wide.region_7.10_spmd.clone.clone.clone.sunk | while | flops 678286848 | bytes 18641908 | solution.py:145
  137.1 1.3 constant_dynamic-slice_fusion.7
  142.5 1.3 constant_dynamic-slice_fusion.7
  147.8 1.3 constant_dynamic-slice_fusion.7
  153.2 1.3 constant_dynamic-slice_fusion.7
  158.6 1.3 constant_dynamic-slice_fusion.7
  164.0 1.3 constant_dynamic-slice_fusion.7
  169.4 1.3 constant_dynamic-slice_fusion.7
  174.8 1.3 constant_dynamic-slice_fusion.7
  179.7 5.7 %slice_bitcast_fusion = (bf16[4096,4,128]{2,0,1:T(8,128)(2,1)}, bf16[4096,4,128]{2,0,1:T(8,128)(2,1)}) fusion(bf16[2,4096,4,128]{3,1,2,0:T(8,128)(2,1)} %get-tuple-element.567), kind=kLoop, calls=%fused_computation.121 | loop fusion | bytes 16777216 | tf_op jit(solution)/shard_map/convert_element_type | solution.py:151
  187.0 6.4 %all-to-all-start.3 = ((bf16[8,32,512]{2,1,0:T(8,128)(2,1)}), bf16[8,32,512]{2,1,0:T(8,128)(2,1)S(1)}, u32[]{:S(2)}, u32[]{:S(2)}) async-start(bf16[8,32,512]{2,1,0:T(8,128)(2,1)} %all_to_all.113), calls=%async_computation.3 | async-start | bytes 524288 | tf_op jit(solution)/shard_map/all_to_all | solution.py:159
  194.4 8.1 %all-to-all-done.3 = bf16[8,32,512]{2,1,0:T(8,128)(2,1)S(1)} async-done(((bf16[8,32,512]{2,1,0:T(8,128)(2,1)}), bf16[8,32,512]{2,1,0:T(8,128)(2,1)S(1)}, u32[]{:S(2)}, u32[]{:S(2)}) %all-to-all-start.3) | async-done | bytes 262176 | tf_op jit(solution)/shard_map/all_to_all | solution.py:159
  202.5 3.4 all-to-all-start.5
  205.9 50.0 %reduce-scatter.3.cloned.1.call-done = bf16[256,4,128]{2,0,1:T(8,128)(2,1)} async-done(((bf16[4096,4,128]{2,0,1:T(8,128)(2,1)}), bf16[256,4,128]{2,0,1:T(8,128)(2,1)}) %reduce-scatter.3.cloned.1.call-update) | async-done | bytes 262160 | tf_op jit(solution)/shard_map/reduce_scatter | solution.py:147
  257.8 7.6 %all-to-all-start.6 = ((bf16[8,32,512]{2,1,0:T(8,128)(2,1)}), bf16[8,32,512]{2,1,0:T(8,128)(2,1)S(1)}, u32[]{:S(2)}, u32[]{:S(2)}) async-start(bf16[8,32,512]{2,1,0:T(8,128)(2,1)} %all_to_all.124), calls=%async_computation.7 | async-start | bytes 524288 | tf_op jit(solution)/shard_map/all_to_all | solution.py:161
  265.5 60.2 %reduce-scatter.5.cloned.1.call-done = bf16[256,4,128]{2,0,1:T(8,128)(2,1)} async-done(((bf16[4096,4,128]{2,0,1:T(8,128)(2,1)}), bf16[256,4,128]{2,0,1:T(8,128)(2,1)}) %reduce-scatter.5.cloned.1.call-update) | async-done | bytes 262160 | tf_op jit(solution)/shard_map/reduce_scatter | solution.py:150
  327.6 6.4 %all-to-all-start.7 = ((bf16[8,32,512]{2,1,0:T(8,128)(2,1)}), bf16[8,32,512]{2,1,0:T(8,128)(2,1)S(1)}, u32[]{:S(2)}, u32[]{:S(2)}) async-start(bf16[8,32,512]{2,1,0:T(8,128)(2,1)} %all_to_all.128), calls=%async_computation.9 | async-start | bytes 524288 | tf_op jit(solution)/shard_map/all_to_all | solution.py:162
  336.2 6.6 %all-to-all-done.7 = bf16[8,32,512]{2,1,0:T(8,128)(2,1)S(1)} async-done(((bf16[8,32,512]{2,1,0:T(8,128)(2,1)}), bf16[8,32,512]{2,1,0:T(8,128)(2,1)S(1)}, u32[]{:S(2)}, u32[]{:S(2)}) %all-to-all-start.7) | async-done | bytes 262176 | tf_op jit(solution)/shard_map/all_to_all | solution.py:162
  (257 shorter events, 73.0 us)
Async XLA Ops:
  7.2 29.8 %copy-start = (bf16[32,4096]{1,0:T(8,128)(2,1)S(1)}, bf16[32,4096]{1,0:T(8,128)(2,1)}, u32[]{:S(2)}) copy-start(bf16[32,4096]{1,0:T(8,128)(2,1)} %param.9) | copy-start | bytes 786436
  8.9 32.2 %copy-start.1 = (bf16[32,4096]{1,0:T(8,128)(2,1)S(1)}, bf16[32,4096]{1,0:T(8,128)(2,1)}, u32[]{:S(2)}) copy-start(bf16[32,4096]{1,0:T(8,128)(2,1)} %param.12) | copy-start | bytes 786436
  8.9 15.9 %all-to-all-start = ((bf16[32,8,512]{2,0,1:T(8,128)(2,1)}), bf16[32,8,512]{2,0,1:T(8,128)(2,1)S(1)}, u32[]{:S(2)}, u32[]{:S(2)}) async-start(bf16[32,8,512]{2,0,1:T(8,128)(2,1)} %bitcast.94), calls=%async_computation | async-start | bytes 524288 | tf_op jit(solution)/shard_map/all_to_all | solution.py:83
  16.1 74.0 %all-gather.2.cloned.1.call-start = ((), (), s32[]{:S(2)}) async-start(), calls=%async_computation.10 | async-start | bytes 8912896 | tf_op jit(solution)/shard_map/all_gather | solution.py:109
  37.7 12.1 %all-to-all-start.2 = ((bf16[32,8,512]{2,0,1:T(8,128)(2,1)}), bf16[32,8,512]{2,0,1:T(8,128)(2,1)S(1)}, u32[]{:S(2)}, u32[]{:S(2)}) async-start(bf16[32,8,512]{2,0,1:T(8,128)(2,1)} %bitcast.92), calls=%async_computation.2 | async-start | bytes 524288 | tf_op jit(solution)/shard_map/all_to_all | solution.py:82
  49.8 14.0 %all-to-all-start.4 = ((bf16[32,8,512]{2,0,1:T(8,128)(2,1)}), bf16[32,8,512]{2,0,1:T(8,128)(2,1)S(1)}, u32[]{:S(2)}, u32[]{:S(2)}) async-start(bf16[32,8,512]{2,0,1:T(8,128)(2,1)} %bitcast.91), calls=%async_computation.4 | async-start | bytes 524288 | tf_op jit(solution)/shard_map/all_to_all | solution.py:85
  53.2 202.7 %reduce-scatter.3.cloned.1.call-start = ((), (), s32[]{:S(2)}) async-start(), calls=%async_computation.11 | async-start | bytes 4456448 | tf_op jit(solution)/shard_map/reduce_scatter | solution.py:147
  63.9 37.5 %copy-start.2 = (s32[32]{0:T(128)S(1)}, s32[32]{0:T(128)}, u32[]{:S(2)}) copy-start(s32[32]{0:T(128)} %param.13) | copy-start | bytes 388
  185.4 140.2 %reduce-scatter.5.cloned.1.call-start = ((), (), s32[]{:S(2)}) async-start(), calls=%async_computation.12 | async-start | bytes 4456448 | tf_op jit(solution)/shard_map/reduce_scatter | solution.py:150
  187.0 15.5 %all-to-all-start.3 = ((bf16[8,32,512]{2,1,0:T(8,128)(2,1)}), bf16[8,32,512]{2,1,0:T(8,128)(2,1)S(1)}, u32[]{:S(2)}, u32[]{:S(2)}) async-start(bf16[8,32,512]{2,1,0:T(8,128)(2,1)} %all_to_all.113), calls=%async_computation.3 | async-start | bytes 524288 | tf_op jit(solution)/shard_map/all_to_all | solution.py:159
  202.5 55.3 %all-to-all-start.5 = ((bf16[8,32,512]{2,1,0:T(8,128)(2,1)}), bf16[8,32,512]{2,1,0:T(8,128)(2,1)S(1)}, u32[]{:S(2)}, u32[]{:S(2)}) async-start(bf16[8,32,512]{2,1,0:T(8,128)(2,1)} %all_to_all.120), calls=%async_computation.5 | async-start | bytes 524288 | tf_op jit(solution)/shard_map/all_to_all | solution.py:160
  257.8 69.8 %all-to-all-start.6 = ((bf16[8,32,512]{2,1,0:T(8,128)(2,1)}), bf16[8,32,512]{2,1,0:T(8,128)(2,1)S(1)}, u32[]{:S(2)}, u32[]{:S(2)}) async-start(bf16[8,32,512]{2,1,0:T(8,128)(2,1)} %all_to_all.124), calls=%async_computation.7 | async-start | bytes 524288 | tf_op jit(solution)/shard_map/all_to_all | solution.py:161
  327.6 15.1 %all-to-all-start.7 = ((bf16[8,32,512]{2,1,0:T(8,128)(2,1)}), bf16[8,32,512]{2,1,0:T(8,128)(2,1)S(1)}, u32[]{:S(2)}, u32[]{:S(2)}) async-start(bf16[8,32,512]{2,1,0:T(8,128)(2,1)} %all_to_all.128), calls=%async_computation.9 | async-start | bytes 524288 | tf_op jit(solution)/shard_map/all_to_all | solution.py:162
Sparse Core Ops, SparseCore 0:
  37.1 52.9 all-gather.1
  185.6 70.2 reduce-scatter.2
  258.3 67.2 reduce-scatter.4
where the time goes:
time: 352 us; the launch traced here: 350 us
  waiting for transfers between devices  178 us (51%)
  local copies, waits for them, and re-layouts  55.3 us (16%)
  starting transfers between devices  38 us (11%)
  matrix products  29.8 us (8%)
  other arithmetic  23 us (7%)
  between operations  13.9 us (4%)
  blocking collectives  11.3 us (3%)
    reduce_scatter x1, waiting for transfers between devices, per_device(): lax.psum_scatter(key_sums[1].astype(jnp.bfloat16), 'ctx', scatter_dimensi...  60.2 us
    reduce_scatter x1, waiting for transfers between devices, per_device(): lax.psum_scatter(key_sums[0].astype(jnp.bfloat16), 'ctx', scatter_dimensi...  50 us
    all_gather x1, waiting for transfers between devices, per_device(): lax.all_gather(jnp.stack((key_here, value_here)), 'ctx', axis=1, tiled=True)  26.2 us
    unnamed x10, local copies, waits for them, and re-layouts  11.5 us
    all_to_all x1, blocking collectives, per_device(): lax.all_to_all(values, 'head', split_axis=1, concat_axis=0, tiled=True)  11.3 us
    all_to_all x1, waiting for transfers between devices, per_device(): lax.all_to_all(grad_out, 'head', split_axis=1, concat_axis=0, tiled=True)  10.4 us
    slice x8, local copies, waits for them, and re-layouts, backward_block(): add_query, add_key, add_value = tile_grads(part[0], part[1], first_row)  10.2 us
    slice x8, local copies, waits for them, and re-layouts, forward_block(): return fold_keys(running, (part[0], part[1]), first_row)  10.2 us
  transfers between devices with their start and end apart: 10, of which 8 were waited for; matrix products, arithmetic and copies ran while one was open for 2% of the time, Pallas kernels for 0%

commit v1 on v0

v1 whole, which is shorter than its diff:
```python
import functools

import jax
import jax.numpy as jnp
from jax import lax
from jax.experimental import pallas as pl
from jax.experimental.pallas import tpu as pltpu
from jax.sharding import Mesh, PartitionSpec as P

HD = 128
BLK = 128
SCALE = HD ** (-0.5)
LOG2E = 1.4426950408889634
NEG = -1e30

N_CC = 8
N_Y = 4
GRP = N_CC * N_Y
ROWS = 32
QB = 256
VM = pltpu.VMEM


def pack_kernel(k_ref, v_ref, q_ref, g_ref, o_ref):
    for a, ref in enumerate((k_ref, v_ref, q_ref, g_ref)):
        for h in range(GRP):
            o_ref[h, a] = ref[:, h * HD : (h + 1) * HD]


def unpack_kernel(x_ref, *o_refs):
    for a, ref in enumerate(o_refs):
        for h in range(GRP):
            ref[:, h * HD : (h + 1) * HD] = x_ref[h, a]


def combine_kernel(outdq_ref, own_ref, recv_ref, o_ref):
    o_ref[:, 0:2] = outdq_ref[...]
    o_ref[:, 2:4] = (own_ref[...] + recv_ref[...].astype(jnp.float32)).astype(jnp.bfloat16)


def dot_nt(a, b):
    return lax.dot_general(a, b, (((1,), (1,)), ((), ())), preferred_element_type=jnp.float32)


def dot_nn(a, b):
    return lax.dot_general(a, b, (((1,), (0,)), ((), ())), preferred_element_type=jnp.float32)


def attention_kernel(
    ids_ref, doc_ref, x_ref, oth_ref,
    outdq_ref, own_ref, sent_ref,
    k_own, v_own, k_oth, v_oth, q_all, g_all, acc,
):
    half, core = ids_ref[0], ids_ref[1]
    lead = jnp.where(half == core, 0, 1)

    def slot(t):
        return jnp.where(half == 1, N_CC - 1 - t, t) * N_Y

    for t in range(N_CC):
        rows = slice(t * BLK, (t + 1) * BLK)
        at = pl.ds(slot(t), N_Y)
        k_own[rows] = x_ref[at, 0].reshape(BLK, HD)
        v_own[rows] = x_ref[at, 1].reshape(BLK, HD)
        q_all[rows] = x_ref[at, 2].reshape(BLK, HD)
        g_all[rows] = x_ref[at, 3].reshape(BLK, HD)
        k_oth[rows] = oth_ref[at, 0].reshape(BLK, HD)
        v_oth[rows] = oth_ref[at, 1].reshape(BLK, HD)

    doc_own = [doc_ref[half * 16 + 2 * t + lead] for t in range(N_CC)]
    doc_oth = [doc_ref[half * 16 + 2 * t + 1 - lead] for t in range(N_CC)]

    row = lax.broadcasted_iota(jnp.int32, (BLK, BLK), 0)
    col = lax.broadcasted_iota(jnp.int32, (BLK, BLK), 1)
    below = col <= row

    def masked(s, u, own):
        tall = []
        for i in range(2):
            t = 2 * u + i
            wide = []
            for tk in range(2 * u + 2):
                tile = s[i * BLK : (i + 1) * BLK, tk * BLK : (tk + 1) * BLK]
                if tk > t:
                    tile = jnp.full_like(tile, NEG)
                elif own and tk == t:
                    tile = jnp.where(below, tile, NEG)
                else:
                    seen = (doc_own if own else doc_oth)[tk] == doc_own[t]
                    if tk == t:
                        seen = seen & (lead == 1)
                    tile = tile + jnp.where(seen, 0.0, NEG)
                wide.append(tile)
            tall.append(jnp.concatenate(wide, axis=1))
        return jnp.concatenate(tall, axis=0)

    for u in reversed(range(N_CC // 2)):
        n = QB * (u + 1)
        first = u == N_CC // 2 - 1
        q = q_all[u * QB : (u + 1) * QB]
        g = g_all[u * QB : (u + 1) * QB]
        s1 = masked(dot_nt(q, k_own[:n]), u, True)
        s2 = masked(dot_nt(q, k_oth[:n]), u, False)
        top = jnp.maximum(
            jnp.max(s1, axis=1, keepdims=True), jnp.max(s2, axis=1, keepdims=True)
        )
        e1 = jnp.exp2((s1 - top) * (SCALE * LOG2E))
        e2 = jnp.exp2((s2 - top) * (SCALE * LOG2E))
        total = jnp.sum(e1, axis=1, keepdims=True) + jnp.sum(e2, axis=1, keepdims=True)
        inv = 1.0 / total
        p1, p2 = e1 * inv, e2 * inv
        b1, b2 = p1.astype(jnp.bfloat16), p2.astype(jnp.bfloat16)
        out = (dot_nn(b1, v_own[:n]) + dot_nn(b2, v_oth[:n])).astype(jnp.bfloat16)
        delta = jnp.sum(g.astype(jnp.float32) * out.astype(jnp.float32), axis=1, keepdims=True)
        d1 = (p1 * (dot_nt(g, v_own[:n]) - delta)).astype(jnp.bfloat16)
        d2 = (p2 * (dot_nt(g, v_oth[:n]) - delta)).astype(jnp.bfloat16)
        dq = ((dot_nn(d1, k_own[:n]) + dot_nn(d2, k_oth[:n])) * SCALE).astype(jnp.bfloat16)
        for i in range(2):
            at = pl.ds(slot(2 * u + i), N_Y)
            part = slice(i * BLK, (i + 1) * BLK)
            outdq_ref[at, 0] = out[part].reshape(N_Y, ROWS, HD)
            outdq_ref[at, 1] = dq[part].reshape(N_Y, ROWS, HD)
        q_t, g_t = q.T, g.T
        for index, left, right in ((0, q_t, d1), (1, g_t, b1), (2, q_t, d2), (3, g_t, b2)):
            new = dot_nn(left, right)
            acc[index, :, :n] = new if first else acc[index, :, :n] + new

    for t in range(N_CC):
        at = pl.ds(slot(t), N_Y)
        cols = slice(t * BLK, (t + 1) * BLK)
        own_ref[at, 0] = (acc[0, :, cols] * SCALE).T.reshape(N_Y, ROWS, HD)
        own_ref[at, 1] = acc[1, :, cols].T.reshape(N_Y, ROWS, HD)
        sent_ref[at, 0] = (acc[2, :, cols] * SCALE).T.astype(jnp.bfloat16).reshape(N_Y, ROWS, HD)
        sent_ref[at, 1] = acc[3, :, cols].T.astype(jnp.bfloat16).reshape(N_Y, ROWS, HD)


def whole(space=VM):
    return pl.BlockSpec(memory_space=space)


def shape(*dims, kind=jnp.bfloat16):
    return jax.ShapeDtypeStruct(dims, kind)


def per_device(queries, keys, values, grad_out, block_doc):
    packed = pl.pallas_call(
        pack_kernel,
        name="pack",
        out_shape=shape(GRP, 4, ROWS, HD),
        in_specs=[whole()] * 4,
        out_specs=whole(),
    )(keys, values, queries, grad_out)
    mine = lax.all_to_all(packed, ("cc", "y"), 0, 0, tiled=True)
    swap = [(0, 1), (1, 0)]
    other = lax.ppermute(mine[:, 0:2], "core", swap)
    ids = jnp.stack([lax.axis_index("xh"), lax.axis_index("core")]).astype(jnp.int32)
    half_rows = N_CC * BLK
    outdq, own, sent = pl.pallas_call(
        attention_kernel,
        name="attention",
        out_shape=(
            shape(GRP, 2, ROWS, HD),
            shape(GRP, 2, ROWS, HD, kind=jnp.float32),
            shape(GRP, 2, ROWS, HD),
        ),
        in_specs=[whole(pltpu.SMEM), whole(pltpu.SMEM), whole(), whole()],
        out_specs=(whole(), whole(), whole()),
        scratch_shapes=[VM((half_rows, HD), jnp.bfloat16)] * 6
        + [VM((4, HD, half_rows), jnp.float32)],
    )(ids, block_doc, mine, other)
    received = lax.ppermute(sent, "core", swap)
    back = pl.pallas_call(
        combine_kernel,
        name="combine",
        out_shape=shape(GRP, 4, ROWS, HD),
        in_specs=[whole()] * 3,
        out_specs=whole(),
    )(outdq, own, received)
    back = lax.all_to_all(back, ("cc", "y"), 0, 0, tiled=True)
    return tuple(
        pl.pallas_call(
            unpack_kernel,
            name="unpack",
            out_shape=(shape(ROWS, GRP * HD),) * 4,
            in_specs=[whole()],
            out_specs=(whole(),) * 4,
        )(back)
    )


def solution(mesh):
    split = Mesh(mesh.devices.reshape(N_CC, 2, 2, N_Y), ("cc", "core", "xh", "y"))
    rows = P(("cc", "core", "xh", "y"), None)
    return jax.shard_map(
        per_device,
        mesh=split,
        in_specs=(rows, rows, rows, rows, P()),
        out_specs=(rows,) * 4,
        check_vma=False,
    )
```

time: 352 us -> 70.3 us (0.20)
  waiting for transfers between devices: 178 us -> 3.16 us
  local copies, waits for them, and re-layouts: 55.3 us -> 1.64 us
  starting transfers between devices: 38 us -> 0.22 us
  blocking collectives: 11.3 us -> 47.8 us
  matrix products: 29.8 us -> 0 us
  other arithmetic: 23 us -> 0.71 us
  Pallas kernels: 0 us -> 15.6 us
  between operations: 13.9 us -> 0.66 us
    reduce_scatter x2 -> x0, waiting for transfers between devices: 110 us -> none  [the longest x1 60.2 us: per_device(): lax.psum_scatter(key_sums[1].astype(jnp.bfloat16), 'ctx', scatter_dimensi...]
    all_to_all x7 -> x0, waiting for transfers between devices: 40.7 us -> none  [the longest x1 10.4 us: per_device(): lax.all_to_all(grad_out, 'head', split_axis=1, concat_axis=0, tiled=True)]
    all_to_all x7 -> x0, starting transfers between devices: 37.9 us -> none  [the longest x1 7.64 us: per_device(): lax.all_to_all(key_flat, 'head', split_axis=0, concat_axis=1, tiled=True)]
    all_to_all x1 -> x2, blocking collectives: 11.3 us -> 47.8 us  [the longest x1 25.9 us: per_device(): mine = lax.all_to_all(packed, ('cc', 'y'), 0, 0, tiled=True)]
    dot_general x56 -> x0, matrix products: 29.8 us -> none  [the longest x8 5.92 us: forward_update(): jnp.einsum('hqk,khd->qhd', shifted.astype(jnp.bfloat16), value_part, pref...]
    all_gather x1 -> x0, waiting for transfers between devices: 26.2 us -> none  [per_device(): lax.all_gather(jnp.stack((key_here, value_here)), 'ctx', axis=1, tiled=True)]
    slice x16 -> x1, local copies, waits for them, and re-layouts: 20.5 us -> 0.04 us  [per_device(): other = lax.ppermute(mine[:, 0:2], 'core', swap)]
    pallas_call x0 -> x4, Pallas kernels: none -> 15.6 us  [the longest x1 8.26 us: per_device(): pl.pallas_call(attention_kernel, name='attention', out_shape=(shape(GRP,...]
  transfers between devices with their start and end apart: 10 -> 2, of which waited for: 8 -> 2; matrix products, arithmetic and copies ran while one was open for 2% -> 1% of each run, Pallas kernels for 0% -> 0%
where the time goes in v1:
time: 70.3 us; the launch traced here: 69.9 us
  blocking collectives  47.8 us (68%)
  Pallas kernels  15.6 us (22%)
  waiting for transfers between devices  3.16 us (4%)
  local copies, waits for them, and re-layouts  1.64 us (2%)
  other arithmetic  0.71 us (1%)
    all_to_all x1, blocking collectives, per_device(): mine = lax.all_to_all(packed, ('cc', 'y'), 0, 0, tiled=True)  25.9 us
    all_to_all x1, blocking collectives, per_device(): back = lax.all_to_all(back, ('cc', 'y'), 0, 0, tiled=True)  22 us
    pallas_call x1, Pallas kernels, per_device(): pl.pallas_call(attention_kernel, name='attention', out_shape=(shape(GRP,...  8.26 us
    pallas_call x1, Pallas kernels, per_device(): pl.pallas_call(combine_kernel, name='combine', out_shape=shape(GRP, 4, RO...  2.66 us
    pallas_call x1, Pallas kernels, per_device(): pl.pallas_call(unpack_kernel, name='unpack', out_shape=(shape(ROWS, GRP *...  2.37 us
    pallas_call x1, Pallas kernels, per_device(): pl.pallas_call(pack_kernel, name='pack', out_shape=shape(GRP, 4, ROWS, HD...  2.34 us
    ppermute x1, waiting for transfers between devices, per_device(): received = lax.ppermute(sent, 'core', swap)  1.98 us
    unnamed x6, local copies, waits for them, and re-layouts  1.61 us
  transfers between devices with their start and end apart: 2, of which 2 were waited for; matrix products, arithmetic and copies ran while one was open for 1% of the time, Pallas kernels for 0%

profile of v1, /device:TPU:0, one launch (start us, length us, event | category | flops | bytes accessed | tf_op | source)
XLA Modules:
  0.0 69.9 jit_solution(3372782754611642517)
XLA Ops:
  0.6 2.3 %pack.1 = bf16[32,4,32,128]{3,2,1,0:T(8,128)(2,1)} custom-call(bf16[32,4096]{1,0:T(8,128)(2,1)} %k_ref.1, bf16[32,4096]{1,0:T(8,128)(2,1)} %v_ref.1, bf16[32,4096]{1,0:T(8,128)(2,1)} %q_ref.1, bf16[32,4096]{1,0:T(8,128)(2,1)} %g_ref.1), custom_call_target="tpu_custom_call" | custom-call | tf_op jit(solution)/shard_map/pack/pallas_call | solution.py:146
  3.0 25.9 %all_to_all.10.x_ref = bf16[32,4,32,128]{3,2,1,0:T(8,128)(2,1)S(1)} all-to-all(bf16[32,4,32,128]{3,2,1,0:T(8,128)(2,1)} %pack.1), channel_id=1, replica_groups=mesh['cc'=8,'core'=2,'xh'=2,'y'=4] {'cc','y'}, dimensions={0} | all-to-all | bytes 2097152 | tf_op jit(solution)/shard_map/all_to_all | solution.py:153
  28.8 0.0 copy-start
  28.9 0.1 collective-permute-start
  29.0 0.7 %pad_add_fusion.ids_ref = s32[2]{0:T(128)} fusion(s32[1]{0:T(128)} %bitcast.1, s32[1]{0:T(128)} %bitcast), kind=kLoop, calls=%fused_computation | loop fusion | flops 2 | bytes 16 | tf_op jit(solution)/shard_map/stack | solution.py:156
  29.7 1.2 %collective-permute-done.oth_ref = bf16[32,2,32,128]{3,2,1,0:T(8,128)(2,1)S(1)} collective-permute-done((bf16[32,2,32,128]{3,2,1,0:T(8,128)(2,1)S(1)}, bf16[32,2,32,128]{3,2,1,0:T(8,128)(2,1)S(1)}, u32[]{:S(2)}, u32[]{:S(2)}) %collective-permute-start) | collective-permute-done | bytes 524320 | tf_op jit(solution)/shard_map/ppermute | solution.py:155
  30.9 0.0 copy-done
  30.9 0.0 copy-start.1
  30.9 0.8 %copy-done.1 = bf16[32,2,32,128]{3,2,1,0:T(8,128)(2,1)} copy-done((bf16[32,2,32,128]{3,2,1,0:T(8,128)(2,1)}, bf16[32,2,32,128]{3,2,1,0:T(8,128)(2,1)S(1)}, u32[]{:S(2)}) %copy-start.1) | copy-done | bytes 524312
  31.7 8.3 %attention.1 = (bf16[32,2,32,128]{3,2,1,0:T(8,128)(2,1)}, f32[32,2,32,128]{3,2,1,0:T(8,128)}, bf16[32,2,32,128]{3,2,1,0:T(8,128)(2,1)}) custom-call(s32[2]{0:T(128)} %pad_add_fusion.ids_ref, s32[32]{0:T(128)} %doc_ref.1, bf16[32,4,32,128]{3,2,1,0:T(8,128)(2,1)} %copy-done, bf16[32,2,32,128]{3,2,1,0:T(8,128)(2,1)} %copy-done.1), custom_call_target="tpu_custom_call" | custom-call | tf_op jit(solution)/shard_map/attention/pallas_call | solution.py:158
  39.9 0.1 collective-permute-start.1
  40.1 2.0 %collective-permute-done.1.recv_ref = bf16[32,2,32,128]{3,2,1,0:T(8,128)(2,1)S(1)} collective-permute-done((bf16[32,2,32,128]{3,2,1,0:T(8,128)(2,1)}, bf16[32,2,32,128]{3,2,1,0:T(8,128)(2,1)S(1)}, u32[]{:S(2)}, u32[]{:S(2)}) %collective-permute-start.1) | collective-permute-done | bytes 524320 | tf_op jit(solution)/shard_map/ppermute | solution.py:171
  42.1 0.0 copy-start.2
  42.1 0.8 %copy-done.2 = bf16[32,2,32,128]{3,2,1,0:T(8,128)(2,1)} copy-done((bf16[32,2,32,128]{3,2,1,0:T(8,128)(2,1)}, bf16[32,2,32,128]{3,2,1,0:T(8,128)(2,1)S(1)}, u32[]{:S(2)}) %copy-start.2) | copy-done | bytes 524312
  42.9 2.7 %combine.1 = bf16[32,4,32,128]{3,2,1,0:T(8,128)(2,1)} custom-call(bf16[32,2,32,128]{3,2,1,0:T(8,128)(2,1)} %get-tuple-element.7.outdq_ref, f32[32,2,32,128]{3,2,1,0:T(8,128)} %get-tuple-element.8.own_ref, bf16[32,2,32,128]{3,2,1,0:T(8,128)(2,1)} %copy-done.2), custom_call_target="tpu_custom_call" | custom-call | tf_op jit(solution)/shard_map/combine/pallas_call | solution.py:172
  45.5 22.0 %all_to_all.11.x_ref = bf16[32,4,32,128]{3,2,1,0:T(8,128)(2,1)} all-to-all(bf16[32,4,32,128]{3,2,1,0:T(8,128)(2,1)} %combine.1), channel_id=1, replica_groups=mesh['cc'=8,'core'=2,'xh'=2,'y'=4] {'cc','y'}, dimensions={0} | all-to-all | bytes 2097152 | tf_op jit(solution)/shard_map/all_to_all | solution.py:179
  67.5 2.4 %unpack.1 = (bf16[32,4096]{1,0:T(8,128)(2,1)}, bf16[32,4096]{1,0:T(8,128)(2,1)}, bf16[32,4096]{1,0:T(8,128)(2,1)}, bf16[32,4096]{1,0:T(8,128)(2,1)}) custom-call(bf16[32,4,32,128]{3,2,1,0:T(8,128)(2,1)} %all_to_all.11.x_ref), custom_call_target="tpu_custom_call" | custom-call | tf_op jit(solution)/shard_map/unpack/pallas_call | solution.py:181
  (1 shorter events, 0.0 us)
Async XLA Ops:
  28.8 2.0 %copy-start = (bf16[32,4,32,128]{3,2,1,0:T(8,128)(2,1)}, bf16[32,4,32,128]{3,2,1,0:T(8,128)(2,1)S(1)}, u32[]{:S(2)}) copy-start(bf16[32,4,32,128]{3,2,1,0:T(8,128)(2,1)S(1)} %all_to_all.10.x_ref) | copy-start | bytes 3145732
  28.9 2.0 %collective-permute-start = (bf16[32,2,32,128]{3,2,1,0:T(8,128)(2,1)S(1)}, bf16[32,2,32,128]{3,2,1,0:T(8,128)(2,1)S(1)}, u32[]{:S(2)}, u32[]{:S(2)}) collective-permute-start(bf16[32,2,32,128]{3,2,1,0:T(8,128)(2,1)S(1)} %slice.4), channel_id=1, source_target_pairs={{0,8},{8,0},{1,9},{9,1},{2,10},{10,2},{3,11},{11,3},{4,12},{12,4},... | collective-permute-start | bytes 1572872 | tf_op jit(solution)/shard_map/ppermute | solution.py:155
  30.9 0.8 %copy-start.1 = (bf16[32,2,32,128]{3,2,1,0:T(8,128)(2,1)}, bf16[32,2,32,128]{3,2,1,0:T(8,128)(2,1)S(1)}, u32[]{:S(2)}) copy-start(bf16[32,2,32,128]{3,2,1,0:T(8,128)(2,1)S(1)} %collective-permute-done.oth_ref) | copy-start | bytes 1572868
  39.9 2.1 %collective-permute-start.1 = (bf16[32,2,32,128]{3,2,1,0:T(8,128)(2,1)}, bf16[32,2,32,128]{3,2,1,0:T(8,128)(2,1)S(1)}, u32[]{:S(2)}, u32[]{:S(2)}) collective-permute-start(bf16[32,2,32,128]{3,2,1,0:T(8,128)(2,1)} %get-tuple-element.9), channel_id=1, source_target_pairs={{0,8},{8,0},{1,9},{9,1},{2,10},{10,2},{3,11},{11,3},{4,12},{12,4},... | collective-permute-start | bytes 1572872 | tf_op jit(solution)/shard_map/ppermute | solution.py:171
  42.1 0.8 %copy-start.2 = (bf16[32,2,32,128]{3,2,1,0:T(8,128)(2,1)}, bf16[32,2,32,128]{3,2,1,0:T(8,128)(2,1)S(1)}, u32[]{:S(2)}) copy-start(bf16[32,2,32,128]{3,2,1,0:T(8,128)(2,1)S(1)} %collective-permute-done.1.recv_ref) | copy-start | bytes 1572868

commit v2 on v1

--- a/solution.py
+++ b/solution.py
@@ -21,16 +21,30 @@
 VM = pltpu.VMEM
 
 
-def pack_kernel(k_ref, v_ref, q_ref, g_ref, o_ref):
-    for a, ref in enumerate((k_ref, v_ref, q_ref, g_ref)):
+def pack_kernel(k_ref, v_ref, q_ref, g_ref, o_ref, buf, sems):
+    copies = [
+        pltpu.make_async_copy(ref, buf.at[a], sems.at[a])
+        for a, ref in enumerate((k_ref, v_ref, q_ref, g_ref))
+    ]
+    for copy in copies:
+        copy.start()
+    for a, copy in enumerate(copies):
+        copy.wait()
         for h in range(GRP):
-            o_ref[h, a] = ref[:, h * HD : (h + 1) * HD]
-
-
-def unpack_kernel(x_ref, *o_refs):
-    for a, ref in enumerate(o_refs):
+            o_ref[h, a] = buf[a, :, h * HD : (h + 1) * HD]
+
+
+def unpack_kernel(x_ref, o0_ref, o1_ref, o2_ref, o3_ref, buf, sems):
+    copies = [
+        pltpu.make_async_copy(buf.at[a], ref, sems.at[a])
+        for a, ref in enumerate((o0_ref, o1_ref, o2_ref, o3_ref))
+    ]
+    for a, copy in enumerate(copies):
         for h in range(GRP):
-            ref[:, h * HD : (h + 1) * HD] = x_ref[h, a]
+            buf[a, :, h * HD : (h + 1) * HD] = x_ref[h, a]
+        copy.start()
+    for copy in copies:
+        copy.wait()
 
 
 def combine_kernel(outdq_ref, own_ref, recv_ref, o_ref):
@@ -47,11 +61,11 @@
 
 
 def attention_kernel(
-    ids_ref, doc_ref, x_ref, oth_ref,
+    doc_ref, x_ref, oth_ref,
     outdq_ref, own_ref, sent_ref,
     k_own, v_own, k_oth, v_oth, q_all, g_all, acc,
 ):
-    half, core = ids_ref[0], ids_ref[1]
+    half, core = lax.axis_index("xh"), lax.axis_index("core")
     lead = jnp.where(half == core, 0, 1)
 
     def slot(t):
@@ -142,49 +156,74 @@
     return jax.ShapeDtypeStruct(dims, kind)
 
 
+def near(*dims, kind=jnp.bfloat16):
+    return VM(dims, kind)
+
+
+def far(x):
+    return pltpu.with_memory_space_constraint(x, pltpu.HBM)
+
+
+def grant(mib):
+    return pltpu.CompilerParams(vmem_limit_bytes=mib << 20)
+
+
+def staging():
+    return [VM((4, ROWS, GRP * HD), jnp.bfloat16), pltpu.SemaphoreType.DMA((4,))]
+
+
+def held(x):
+    return pltpu.with_memory_space_constraint(x, VM)
+
+
 def per_device(queries, keys, values, grad_out, block_doc):
     packed = pl.pallas_call(
         pack_kernel,
         name="pack",
-        out_shape=shape(GRP, 4, ROWS, HD),
-        in_specs=[whole()] * 4,
+        compiler_params=grant(8),
+        out_shape=near(GRP, 4, ROWS, HD),
+        in_specs=[whole(pltpu.HBM)] * 4,
         out_specs=whole(),
-    )(keys, values, queries, grad_out)
+        scratch_shapes=staging(),
+    )(*[far(x) for x in (keys, values, queries, grad_out)])
     mine = lax.all_to_all(packed, ("cc", "y"), 0, 0, tiled=True)
     swap = [(0, 1), (1, 0)]
     other = lax.ppermute(mine[:, 0:2], "core", swap)
-    ids = jnp.stack([lax.axis_index("xh"), lax.axis_index("core")]).astype(jnp.int32)
     half_rows = N_CC * BLK
     outdq, own, sent = pl.pallas_call(
         attention_kernel,
         name="attention",
+        compiler_params=grant(40),
         out_shape=(
-            shape(GRP, 2, ROWS, HD),
-            shape(GRP, 2, ROWS, HD, kind=jnp.float32),
-            shape(GRP, 2, ROWS, HD),
+            near(GRP, 2, ROWS, HD),
+            near(GRP, 2, ROWS, HD, kind=jnp.float32),
+            near(GRP, 2, ROWS, HD),
         ),
-        in_specs=[whole(pltpu.SMEM), whole(pltpu.SMEM), whole(), whole()],
+        in_specs=[whole(pltpu.SMEM), whole(), whole()],
         out_specs=(whole(), whole(), whole()),
         scratch_shapes=[VM((half_rows, HD), jnp.bfloat16)] * 6
         + [VM((4, HD, half_rows), jnp.float32)],
-    )(ids, block_doc, mine, other)
+    )(block_doc, held(mine), held(other))
     received = lax.ppermute(sent, "core", swap)
     back = pl.pallas_call(
         combine_kernel,
         name="combine",
-        out_shape=shape(GRP, 4, ROWS, HD),
+        compiler_params=grant(8),
+        out_shape=near(GRP, 4, ROWS, HD),
         in_specs=[whole()] * 3,
         out_specs=whole(),
-    )(outdq, own, received)
+    )(held(outdq), held(own), held(received))
     back = lax.all_to_all(back, ("cc", "y"), 0, 0, tiled=True)
     return tuple(
         pl.pallas_call(
             unpack_kernel,
             name="unpack",
+            compiler_params=grant(8),
             out_shape=(shape(ROWS, GRP * HD),) * 4,
             in_specs=[whole()],
-            out_specs=(whole(),) * 4,
-        )(back)
+            out_specs=(whole(pltpu.HBM),) * 4,
+            scratch_shapes=staging(),
+        )(held(back))
     )
 
 

time: 70.3 us -> 61 us (0.87)
  Pallas kernels: 15.6 us -> 8.74 us
  local copies, waits for them, and re-layouts: 1.64 us -> 0.04 us
  other arithmetic: 0.71 us -> 0 us
    pallas_call x4, Pallas kernels: 15.6 us -> 8.74 us  [the longest x1 6.29 us: per_device(): pl.pallas_call(attention_kernel, name='attention', compiler_params=grant(...]
    unnamed x6 -> x2, local copies, waits for them, and re-layouts: 1.61 us -> 0.01 us
    ppermute x1, waiting for transfers between devices: 1.18 us -> 1.9 us  [per_device(): other = lax.ppermute(mine[:, 0:2], 'core', swap)]
    another operation x1 -> x0, other arithmetic: 0.71 us -> none  [per_device(): jnp.stack([lax.axis_index('xh'), lax.axis_index('core')]).astype(jnp.int32)]
  transfers between devices with their start and end apart: 2 -> 2, of which waited for: 2 -> 2; matrix products, arithmetic and copies ran while one was open for 1% -> 0% of each run, Pallas kernels for 0% -> 0%
where the time goes in v2:
time: 61 us; the launch traced here: 60.7 us
  blocking collectives  47.3 us (78%)
  Pallas kernels  8.74 us (14%)
  waiting for transfers between devices  3.66 us (6%)
  between operations  0.67 us (1%)
    all_to_all x1, blocking collectives, per_device(): mine = lax.all_to_all(packed, ('cc', 'y'), 0, 0, tiled=True)  25.7 us
    all_to_all x1, blocking collectives, per_device(): back = lax.all_to_all(back, ('cc', 'y'), 0, 0, tiled=True)  21.7 us
    pallas_call x1, Pallas kernels, per_device(): pl.pallas_call(attention_kernel, name='attention', compiler_params=grant(...  6.29 us
    ppermute x1, waiting for transfers between devices, per_device(): other = lax.ppermute(mine[:, 0:2], 'core', swap)  1.9 us
    ppermute x1, waiting for transfers between devices, per_device(): received = lax.ppermute(sent, 'core', swap)  1.77 us
    pallas_call x1, Pallas kernels, per_device(): pl.pallas_call(pack_kernel, name='pack', compiler_params=grant(8), out_sh...  1.27 us
  transfers between devices with their start and end apart: 2, of which 2 were waited for; matrix products, arithmetic and copies ran while one was open for 0% of the time, Pallas kernels for 0%

profile of v2, /device:TPU:0, one launch (start us, length us, event | category | flops | bytes accessed | tf_op | source)
XLA Modules:
  0.0 60.7 jit_solution(164925153843493409)
XLA Ops:
  0.6 1.3 %pack.1 = bf16[32,4,32,128]{3,2,1,0:T(8,128)(2,1)S(1)} custom-call(bf16[32,4096]{1,0:T(8,128)(2,1)} %k_ref.1, bf16[32,4096]{1,0:T(8,128)(2,1)} %v_ref.1, bf16[32,4096]{1,0:T(8,128)(2,1)} %q_ref.1, bf16[32,4096]{1,0:T(8,128)(2,1)} %g_ref.1), custom_call_target="tpu_custom_call" | custom-call | tf_op jit(solution)/shard_map/pack/pallas_call | solution.py:180
  1.9 25.7 %all_to_all.10.x_ref = bf16[32,4,32,128]{3,2,1,0:T(8,128)(2,1)S(1)} all-to-all(bf16[32,4,32,128]{3,2,1,0:T(8,128)(2,1)S(1)} %pack.1), channel_id=1, replica_groups=mesh['cc'=8,'core'=2,'xh'=2,'y'=4] {'cc','y'}, dimensions={0} | all-to-all | bytes 2097152 | tf_op jit(solution)/shard_map/all_to_all | solution.py:189
  27.6 0.0 copy-start
  27.6 0.1 collective-permute-start
  27.7 1.9 %collective-permute-done.oth_ref = bf16[32,2,32,128]{3,2,1,0:T(8,128)(2,1)S(1)} collective-permute-done((bf16[32,2,32,128]{3,2,1,0:T(8,128)(2,1)S(1)}, bf16[32,2,32,128]{3,2,1,0:T(8,128)(2,1)S(1)}, u32[]{:S(2)}, u32[]{:S(2)}) %collective-permute-start) | collective-permute-done | bytes 524320 | tf_op jit(solution)/shard_map/ppermute | solution.py:191
  29.6 0.0 copy-done
  29.6 6.3 %attention.1 = (bf16[32,2,32,128]{3,2,1,0:T(8,128)(2,1)S(1)}, f32[32,2,32,128]{3,2,1,0:T(8,128)S(1)}, bf16[32,2,32,128]{3,2,1,0:T(8,128)(2,1)S(1)}) custom-call(s32[32]{0:T(128)S(1)} %copy-done, bf16[32,4,32,128]{3,2,1,0:T(8,128)(2,1)S(1)} %all_to_all.10.x_ref, bf16[32,2,32,128]{3,2,1,0:T(8,128)(2,1)S(1)} %collective-permute-done.oth_ref), custom_call_target="tpu_custom_call" | custom-call | tf_op jit(solution)/shard_map/attention/pallas_call | solution.py:193
  35.9 0.2 collective-permute-start.1
  36.1 1.8 %collective-permute-done.1.recv_ref = bf16[32,2,32,128]{3,2,1,0:T(8,128)(2,1)S(1)} collective-permute-done((bf16[32,2,32,128]{3,2,1,0:T(8,128)(2,1)S(1)}, bf16[32,2,32,128]{3,2,1,0:T(8,128)(2,1)S(1)}, u32[]{:S(2)}, u32[]{:S(2)}) %collective-permute-start.1) | collective-permute-done | bytes 524320 | tf_op jit(solution)/shard_map/ppermute | solution.py:207
  37.9 0.1 combine.1
  38.0 21.7 %all_to_all.11.x_ref = bf16[32,4,32,128]{3,2,1,0:T(8,128)(2,1)S(1)} all-to-all(bf16[32,4,32,128]{3,2,1,0:T(8,128)(2,1)S(1)} %combine.1), channel_id=1, replica_groups=mesh['cc'=8,'core'=2,'xh'=2,'y'=4] {'cc','y'}, dimensions={0} | all-to-all | bytes 2097152 | tf_op jit(solution)/shard_map/all_to_all | solution.py:216
  59.7 1.0 %unpack.1 = (bf16[32,4096]{1,0:T(8,128)(2,1)}, bf16[32,4096]{1,0:T(8,128)(2,1)}, bf16[32,4096]{1,0:T(8,128)(2,1)}, bf16[32,4096]{1,0:T(8,128)(2,1)}) custom-call(bf16[32,4,32,128]{3,2,1,0:T(8,128)(2,1)S(1)} %all_to_all.11.x_ref), custom_call_target="tpu_custom_call" | custom-call | tf_op jit(solution)/shard_map/unpack/pallas_call | solution.py:218
  (1 shorter events, 0.0 us)
Async XLA Ops:
  27.6 2.0 %copy-start = (s32[32]{0:T(128)S(1)}, s32[32]{0:T(128)}, u32[]{:S(2)}) copy-start(s32[32]{0:T(128)} %doc_ref.1) | copy-start | bytes 388
  27.6 2.0 %collective-permute-start = (bf16[32,2,32,128]{3,2,1,0:T(8,128)(2,1)S(1)}, bf16[32,2,32,128]{3,2,1,0:T(8,128)(2,1)S(1)}, u32[]{:S(2)}, u32[]{:S(2)}) collective-permute-start(bf16[32,2,32,128]{3,2,1,0:T(8,128)(2,1)S(1)} %slice.4), channel_id=1, source_target_pairs={{0,8},{8,0},{1,9},{9,1},{2,10},{10,2},{3,11},{11,3},{4,12},{12,4},... | collective-permute-start | bytes 1572872 | tf_op jit(solution)/shard_map/ppermute | solution.py:191
  35.9 2.0 %collective-permute-start.1 = (bf16[32,2,32,128]{3,2,1,0:T(8,128)(2,1)S(1)}, bf16[32,2,32,128]{3,2,1,0:T(8,128)(2,1)S(1)}, u32[]{:S(2)}, u32[]{:S(2)}) collective-permute-start(bf16[32,2,32,128]{3,2,1,0:T(8,128)(2,1)S(1)} %get-tuple-element.9), channel_id=1, source_target_pairs={{0,8},{8,0},{1,9},{9,1},{2,10},{10,2},{3,11},{11,3},{4,12},{12,4},... | collective-permute-start | bytes 1572872 | tf_op jit(solution)/shard_map/ppermute | solution.py:207

commit v3 on v2

v3 whole, which is shorter than its diff:
```python
import functools

import jax
import jax.numpy as jnp
from jax import lax
from jax.experimental import pallas as pl
from jax.experimental.pallas import tpu as pltpu
from jax.sharding import Mesh, PartitionSpec as P

HD = 128
BLK = 128
SCALE = HD ** (-0.5)
LOG2E = 1.4426950408889634
NEG = -1e30

N_CC = 8
N_Y = 4
GRP = N_CC * N_Y
ROWS = 32
QB = 256
RC = 64
VM = pltpu.VMEM


def pack_kernel(k_ref, v_ref, q_ref, g_ref, o_ref, buf, sems):
    copies = [
        pltpu.make_async_copy(ref, buf.at[a], sems.at[a])
        for a, ref in enumerate((k_ref, v_ref, q_ref, g_ref))
    ]
    for copy in copies:
        copy.start()
    for a, copy in enumerate(copies):
        copy.wait()
        for h in range(GRP):
            o_ref[h, a] = buf[a, :, h * HD : (h + 1) * HD]


def unpack_kernel(x_ref, o0_ref, o1_ref, o2_ref, o3_ref, buf, sems):
    copies = [
        pltpu.make_async_copy(buf.at[a], ref, sems.at[a])
        for a, ref in enumerate((o0_ref, o1_ref, o2_ref, o3_ref))
    ]
    for a, copy in enumerate(copies):
        for h in range(GRP):
            buf[a, :, h * HD : (h + 1) * HD] = x_ref[h, a]
        copy.start()
    for copy in copies:
        copy.wait()


def dot_nt(a, b):
    return lax.dot_general(a, b, (((1,), (1,)), ((), ())), preferred_element_type=jnp.float32)


def dot_nn(a, b):
    return lax.dot_general(a, b, (((1,), (0,)), ((), ())), preferred_element_type=jnp.float32)


def placed():
    half, core = lax.axis_index("xh"), lax.axis_index("core")
    lead = jnp.where(half == core, 0, 1)
    slots = [jnp.where(half == 1, N_CC - 1 - t, t) for t in range(N_CC)]
    return half, lead, slots


def masked(s, u, bias):
    tall = []
    for i in range(2):
        wide = [
            bias(2 * u + i, tk, s[i * BLK : (i + 1) * BLK, tk * BLK : (tk + 1) * BLK])
            for tk in range(2 * u + 2)
        ]
        tall.append(jnp.concatenate(wide, axis=1))
    return jnp.concatenate(tall, axis=0)


def rows_of(u):
    return slice(u * QB, (u + 1) * QB)


def chunks(u):
    return [(low, slice(u * QB + low, u * QB + low + RC)) for low in range(0, QB, RC)]


def joined(parts):
    return [jnp.concatenate(column, axis=0) for column in zip(*parts)]


def own_kernel(doc_ref, x_ref, all_ref, e_ref, w_ref, m_ref, l_ref):
    half, lead, slots = placed()
    for t in range(N_CC):
        for a in range(4):
            all_ref[a, t * BLK : (t + 1) * BLK] = x_ref[:, slots[t], a].reshape(BLK, HD)
    doc = [doc_ref[half * 16 + 2 * t + lead] for t in range(N_CC)]
    below = lax.broadcasted_iota(jnp.int32, (BLK, BLK), 1) <= lax.broadcasted_iota(
        jnp.int32, (BLK, BLK), 0
    )

    def bias(t, tk, tile):
        if tk > t:
            return jnp.full_like(tile, NEG)
        if tk == t:
            return jnp.where(below, tile, NEG)
        return tile + jnp.where(doc[tk] == doc[t], 0.0, NEG)

    for u in reversed(range(N_CC // 2)):
        n, r = QB * (u + 1), rows_of(u)
        s = masked(dot_nt(all_ref[2, r], all_ref[0, :n]), u, bias)
        w_ref[r, :n] = dot_nt(all_ref[3, r], all_ref[1, :n])
        for low, part in chunks(u):
            piece = s[low : low + RC]
            top = jnp.max(piece, axis=1, keepdims=True)
            e = jnp.exp2((piece - top) * (SCALE * LOG2E))
            e_ref[part, :n] = e
            m_ref[part] = jnp.broadcast_to(top, (RC, HD))
            l_ref[part] = jnp.broadcast_to(jnp.sum(e, axis=1, keepdims=True), (RC, HD))


def other_kernel(
    doc_ref, all_ref, oth_ref, e_ref, w_ref, m_ref, l_ref,
    out_ref, sent_ref, b_ref, d_ref, k_ref, v_oth, acc,
):
    half, lead, slots = placed()
    for t in range(N_CC):
        k_ref[t * BLK : (t + 1) * BLK] = oth_ref[:, slots[t], 0].reshape(BLK, HD)
        v_oth[t * BLK : (t + 1) * BLK] = oth_ref[:, slots[t], 1].reshape(BLK, HD)
    doc_own = [doc_ref[half * 16 + 2 * t + lead] for t in range(N_CC)]
    doc_oth = [doc_ref[half * 16 + 2 * t + 1 - lead] for t in range(N_CC)]

    def bias(t, tk, tile):
        if tk > t:
            return jnp.full_like(tile, NEG)
        seen = doc_oth[tk] == doc_own[t]
        if tk == t:
            seen = seen & (lead == 1)
        return tile + jnp.where(seen, 0.0, NEG)

    last = N_CC // 2 - 1

    def scores(u):
        n, r = QB * (u + 1), rows_of(u)
        return dot_nt(all_ref[2, r], k_ref[:n]), dot_nt(all_ref[3, r], v_oth[:n])

    def softmax(u, s):
        n = QB * (u + 1)
        s = masked(s, u, bias)
        parts = []
        for low, part in chunks(u):
            piece = s[low : low + RC]
            m_own = m_ref[part, :1]
            top = jnp.maximum(m_own, jnp.max(piece, axis=1, keepdims=True))
            e = jnp.exp2((piece - top) * (SCALE * LOG2E))
            fade = jnp.exp2((m_own - top) * (SCALE * LOG2E))
            inv = 1.0 / (l_ref[part, :1] * fade + jnp.sum(e, axis=1, keepdims=True))
            p1, p2 = e_ref[part, :n] * (fade * inv), e * inv
            parts.append((p1, p2, p1.astype(jnp.bfloat16), p2.astype(jnp.bfloat16)))
        p1, p2, b1, b2 = joined(parts)
        b_ref[rows_of(u), :n] = b1
        return p1, p2, b1, b2

    def output(u, b1, b2):
        n = QB * (u + 1)
        out = (dot_nn(b1, all_ref[1, :n]) + dot_nn(b2, v_oth[:n])).astype(jnp.bfloat16)
        for i in range(2):
            out_ref[:, slots[2 * u + i]] = out[i * BLK : (i + 1) * BLK].reshape(N_Y, ROWS, HD)
        return out

    def score_grads(u, p1, p2, w, out):
        n = QB * (u + 1)
        parts = []
        for low, part in chunks(u):
            some = slice(low, low + RC)
            g = all_ref[3, part].astype(jnp.float32)
            delta = jnp.sum(g * out[some].astype(jnp.float32), axis=1, keepdims=True)
            d2 = (p2[some] * (w[some] - delta)).astype(jnp.bfloat16)
            d_ref[0, part, :n] = (p1[some] * (w_ref[part, :n] - delta)).astype(jnp.bfloat16)
            d_ref[1, part, :n] = d2
            parts.append((d2,))
        return joined(parts)[0]

    def key_grads(u, d2, b2):
        n, r = QB * (u + 1), rows_of(u)
        for a, left, right in ((0, all_ref[2, r].T, d2), (1, all_ref[3, r].T, b2)):
            new = dot_nn(left, right)
            if u < last:
                new = acc[a, :, :n] + new
            if u:
                acc[a, :, : n - QB] = new[:, : n - QB]
            done = (new[:, n - QB :] * (1.0 if a else SCALE)).astype(jnp.bfloat16).T
            for i in range(2):
                part = done[i * BLK : (i + 1) * BLK].reshape(N_Y, ROWS, HD)
                sent_ref[:, slots[2 * u + i], a] = part

    ready = scores(last)
    before = None
    for u in reversed(range(-1, last + 1)):
        s, w = ready
        if u > 0:
            ready = scores(u - 1)
        if before is not None:
            p1, p2, b2, w_b, out = before
            d2 = score_grads(u + 1, p1, p2, w_b, out)
        if u >= 0:
            q1, q2, c1, c2 = softmax(u, s)
        if before is not None:
            key_grads(u + 1, d2, b2)
        if u >= 0:
            before = q1, q2, c2, w, output(u, c1, c2)


def rest_kernel(all_ref, k_ref, b_ref, d_ref, dq_ref, own_ref):
    _, _, slots = placed()
    q_t, g_t = all_ref[2].T, all_ref[3].T
    for u in reversed(range(N_CC // 2)):
        n, r = QB * (u + 1), rows_of(u)
        dq = dot_nn(d_ref[0, r, :n], all_ref[0, :n]) + dot_nn(d_ref[1, r, :n], k_ref[:n])
        dq = (dq * SCALE).astype(jnp.bfloat16)
        low = u * QB
        dk = dot_nn(q_t[:, low:], d_ref[0, low:, r]) * SCALE
        dv = dot_nn(g_t[:, low:], b_ref[low:, r])
        for i in range(2):
            at, part = slots[2 * u + i], slice(i * BLK, (i + 1) * BLK)
            dq_ref[:, at] = dq[part].reshape(N_Y, ROWS, HD)
            own_ref[:, at, 0] = dk[:, part].T.reshape(N_Y, ROWS, HD)
            own_ref[:, at, 1] = dv[:, part].T.reshape(N_Y, ROWS, HD)


def combine_kernel(out_ref, dq_ref, own_ref, recv_ref, o_ref):
    o_ref[:, :, 0] = out_ref[...]
    o_ref[:, :, 1] = dq_ref[...]
    o_ref[:, :, 2:4] = (own_ref[...] + recv_ref[...].astype(jnp.float32)).astype(jnp.bfloat16)


def whole(space=VM):
    return pl.BlockSpec(memory_space=space)


def shape(*dims, kind=jnp.bfloat16):
    return jax.ShapeDtypeStruct(dims, kind)


def near(*dims, kind=jnp.bfloat16):
    return VM(dims, kind)


def far(x):
    return pltpu.with_memory_space_constraint(x, pltpu.HBM)


def grant(mib):
    return pltpu.CompilerParams(vmem_limit_bytes=mib << 20)


def staging():
    return [VM((4, ROWS, GRP * HD), jnp.bfloat16), pltpu.SemaphoreType.DMA((4,))]


def held(x):
    return pltpu.with_memory_space_constraint(x, VM)


def per_device(queries, keys, values, grad_out, block_doc):
    packed = pl.pallas_call(
        pack_kernel,
        name="pack",
        compiler_params=grant(8),
        out_shape=near(GRP, 4, ROWS, HD),
        in_specs=[whole(pltpu.HBM)] * 4,
        out_specs=whole(),
        scratch_shapes=staging(),
    )(*[far(x) for x in (keys, values, queries, grad_out)])
    mine = lax.all_to_all(packed, ("y", "cc"), 0, 0, tiled=True)
    swap = [(0, 1), (1, 0)]
    mine = mine.reshape(N_Y, N_CC, 4, ROWS, HD)
    other = lax.ppermute(mine[:, :, 0:2], "core", swap)
    smem = whole(pltpu.SMEM)
    full = N_CC * BLK
    f32 = jnp.float32
    everything, exps, weights, top, total = pl.pallas_call(
        own_kernel,
        name="own_keys",
        compiler_params=grant(16),
        out_shape=(
            near(4, full, HD),
            near(full, full, kind=f32),
            near(full, full, kind=f32),
            near(full, HD, kind=f32),
            near(full, HD, kind=f32),
        ),
        in_specs=[smem, whole()],
        out_specs=(whole(),) * 5,
    )(block_doc, held(mine))
    out, sent, probs, grads, k_other = pl.pallas_call(
        other_kernel,
        name="other_keys",
        compiler_params=grant(24),
        out_shape=(
            near(N_Y, N_CC, ROWS, HD),
            near(N_Y, N_CC, 2, ROWS, HD),
            near(full, full),
            near(2, full, full),
            near(full, HD),
        ),
        in_specs=[smem] + [whole()] * 6,
        out_specs=(whole(),) * 5,
        scratch_shapes=[VM((full, HD), jnp.bfloat16), VM((2, HD, full), f32)],
    )(block_doc, *[held(x) for x in (everything, other, exps, weights, top, total)])
    received = lax.ppermute(sent, "core", swap)
    dq, own = pl.pallas_call(
        rest_kernel,
        name="rest",
        compiler_params=grant(16),
        out_shape=(near(N_Y, N_CC, ROWS, HD), near(N_Y, N_CC, 2, ROWS, HD, kind=f32)),
        in_specs=[whole()] * 4,
        out_specs=(whole(),) * 2,
    )(*[held(x) for x in (everything, k_other, probs, grads)])
    back = pl.pallas_call(
        combine_kernel,
        name="combine",
        compiler_params=grant(8),
        out_shape=near(N_Y, N_CC, 4, ROWS, HD),
        in_specs=[whole()] * 4,
        out_specs=whole(),
    )(held(out), held(dq), held(own), held(received))
    back = lax.all_to_all(back.reshape(GRP, 4, ROWS, HD), ("y", "cc"), 0, 0, tiled=True)
    return tuple(
        pl.pallas_call(
            unpack_kernel,
            name="unpack",
            compiler_params=grant(8),
            out_shape=(shape(ROWS, GRP * HD),) * 4,
            in_specs=[whole()],
            out_specs=(whole(pltpu.HBM),) * 4,
            scratch_shapes=staging(),
        )(held(back))
    )


def solution(mesh):
    split = Mesh(mesh.devices.reshape(N_CC, 2, 2, N_Y), ("cc", "core", "xh", "y"))
    rows = P(("cc", "core", "xh", "y"), None)
    return jax.shard_map(
        per_device,
        mesh=split,
        in_specs=(rows, rows, rows, rows, P()),
        out_specs=(rows,) * 4,
        check_vma=False,
    )
```

time: 61 us -> 59.3 us (0.972)
  waiting for transfers between devices: 3.66 us -> 0.53 us
  Pallas kernels: 8.74 us -> 10.3 us
    ppermute x1, waiting for transfers between devices: 1.9 us -> 0.22 us  [per_device(): other = lax.ppermute(mine[:, :, 0:2], 'core', swap)]
    pallas_call x1 -> x3, Pallas kernels: 6.29 us -> 7.86 us  [the longest x1 4.89 us: per_device(): pl.pallas_call(other_kernel, name='other_keys', compiler_params=grant(24)...]
    ppermute x1, waiting for transfers between devices: 1.77 us -> 0.32 us  [per_device(): received = lax.ppermute(sent, 'core', swap)]
  transfers between devices with their start and end apart: 2 -> 2, of which waited for: 2 -> 2; matrix products, arithmetic and copies ran while one was open for 0% -> 0% of each run, Pallas kernels for 0% -> 5%
where the time goes in v3:
time: 59.3 us; the launch traced here: 59 us
  blocking collectives  47 us (79%)
  Pallas kernels  10.3 us (17%)
  between operations  0.71 us (1%)
    all_to_all x1, blocking collectives, per_device(): mine = lax.all_to_all(packed, ('y', 'cc'), 0, 0, tiled=True)  25.5 us
    all_to_all x1, blocking collectives, per_device(): lax.all_to_all(back.reshape(GRP, 4, ROWS, HD), ('y', 'cc'), 0, 0, tiled=T...  21.5 us
    pallas_call x1, Pallas kernels, per_device(): pl.pallas_call(other_kernel, name='other_keys', compiler_params=grant(24)...  4.89 us
    pallas_call x1, Pallas kernels, per_device(): pl.pallas_call(own_kernel, name='own_keys', compiler_params=grant(16), ou...  1.66 us
    pallas_call x1, Pallas kernels, per_device(): pl.pallas_call(rest_kernel, name='rest', compiler_params=grant(16), out_s...  1.3 us
    pallas_call x1, Pallas kernels, per_device(): pl.pallas_call(pack_kernel, name='pack', compiler_params=grant(8), out_sh...  1.27 us
  transfers between devices with their start and end apart: 2, of which 2 were waited for; matrix products, arithmetic and copies ran while one was open for 0% of the time, Pallas kernels for 5%

profile of v3, /device:TPU:0, one launch (start us, length us, event | category | flops | bytes accessed | tf_op | source)
XLA Modules:
  0.0 59.0 jit_solution(13075937237543362814)
XLA Ops:
  0.6 0.0 copy-start
  0.6 1.3 %pack.1 = bf16[32,4,32,128]{3,2,1,0:T(8,128)(2,1)S(1)} custom-call(bf16[32,4096]{1,0:T(8,128)(2,1)} %k_ref.1, bf16[32,4096]{1,0:T(8,128)(2,1)} %v_ref.1, bf16[32,4096]{1,0:T(8,128)(2,1)} %q_ref.1, bf16[32,4096]{1,0:T(8,128)(2,1)} %g_ref.1), custom_call_target="tpu_custom_call" | custom-call | tf_op jit(solution)/shard_map/pack/pallas_call | solution.py:263
  1.9 25.5 %all_to_all.10 = bf16[32,4,32,128]{3,2,1,0:T(8,128)(2,1)S(1)} all-to-all(bf16[32,4,32,128]{3,2,1,0:T(8,128)(2,1)S(1)} %pack.1), channel_id=1, replica_groups=mesh['cc'=8,'core'=2,'xh'=2,'y'=4] {'y','cc'}, dimensions={0} | all-to-all | bytes 2097152 | tf_op jit(solution)/shard_map/all_to_all | solution.py:272
  27.5 0.1 collective-permute-start
  27.6 0.0 copy-done
  27.6 1.7 %own_keys.1 = (bf16[4,1024,128]{2,1,0:T(8,128)(2,1)S(1)}, f32[1024,1024]{1,0:T(8,128)S(1)}, f32[1024,1024]{1,0:T(8,128)S(1)}, f32[1024,128]{1,0:T(8,128)S(1)}, f32[1024,128]{1,0:T(8,128)S(1)}) custom-call(s32[32]{0:T(128)S(1)} %copy-done, bf16[4,8,4,32,128]{4,3,2,1,0:T(8,128)(2,1)S(1)} %bitcast.3), custom_call_target="tpu_custom_call" | custom-call | tf_op jit(solution)/shard_map/own_keys/pallas_call | solution.py:279
  29.3 0.2 collective-permute-done.oth_ref
  29.5 4.9 %other_keys.1 = (bf16[4,8,32,128]{3,2,1,0:T(8,128)(2,1)S(1)}, bf16[4,8,2,32,128]{4,3,2,1,0:T(8,128)(2,1)S(1)}, bf16[1024,1024]{1,0:T(8,128)(2,1)S(1)}, bf16[2,10...) custom-call(s32[32]{0:T(128)S(1)} %copy-done, bf16[4,1024,128]{2,1,0:T(8,128)(2,1)S(1)} %get-tuple-element.16.all_ref, ...), custom_call_target="tpu_custom_call" | custom-call | tf_op jit(solution)/shard_map/other_keys/pallas_call | solution.py:293
  34.4 0.4 collective-permute-start.1
  34.8 1.3 %rest.1 = (bf16[4,8,32,128]{3,2,1,0:T(8,128)(2,1)S(1)}, f32[4,8,2,32,128]{4,3,2,1,0:T(8,128)S(1)}) custom-call(bf16[4,1024,128]{2,1,0:T(8,128)(2,1)S(1)} %get-tuple-element.16.all_ref, bf16[1024,128]{1,0:T(8,128)(2,1)S(1)} %get-tuple-element.22.k_ref, bf16[1024,1024]{1,0:T(8,128)(2,1)S(1)} %get-tuple-element.23.b_ref, ...), custom_call_target="tpu_custom_call" | custom-call | tf_op jit(solution)/shard_map/rest/pallas_call | solution.py:309
  36.1 0.3 collective-permute-done.1.recv_ref
  36.4 0.1 combine.1
  36.5 21.5 %all_to_all.11.x_ref = bf16[32,4,32,128]{3,2,1,0:T(8,128)(2,1)S(1)} all-to-all(bf16[32,4,32,128]{3,2,1,0:T(8,128)(2,1)S(1)} %bitcast.4), channel_id=1, replica_groups=mesh['cc'=8,'core'=2,'xh'=2,'y'=4] {'y','cc'}, dimensions={0} | all-to-all | bytes 2097152 | tf_op jit(solution)/shard_map/all_to_all | solution.py:325
  58.0 1.0 %unpack.1 = (bf16[32,4096]{1,0:T(8,128)(2,1)}, bf16[32,4096]{1,0:T(8,128)(2,1)}, bf16[32,4096]{1,0:T(8,128)(2,1)}, bf16[32,4096]{1,0:T(8,128)(2,1)}) custom-call(bf16[32,4,32,128]{3,2,1,0:T(8,128)(2,1)S(1)} %all_to_all.11.x_ref), custom_call_target="tpu_custom_call" | custom-call | tf_op jit(solution)/shard_map/unpack/pallas_call | solution.py:327
  (1 shorter events, 0.0 us)
Async XLA Ops:
  0.6 27.0 %copy-start = (s32[32]{0:T(128)S(1)}, s32[32]{0:T(128)}, u32[]{:S(2)}) copy-start(s32[32]{0:T(128)} %doc_ref.3) | copy-start | bytes 388
  27.5 2.0 %collective-permute-start = (bf16[4,8,2,32,128]{4,3,2,1,0:T(8,128)(2,1)S(1)}, bf16[4,8,2,32,128]{4,3,2,1,0:T(8,128)(2,1)S(1)}, u32[]{:S(2)}, u32[]{:S(2)}) collective-permute-start(bf16[4,8,2,32,128]{4,3,2,1,0:T(8,128)(2,1)S(1)} %slice.4), channel_id=1, source_target_pairs={{0,8},{8,0},{1,9},{9,1},{2,10},{10,2},{3,11},{11,3},{4,12},{12,4},... | collective-permute-start | bytes 1572872 | tf_op jit(solution)/shard_map/ppermute | solution.py:275
  34.4 2.0 %collective-permute-start.1 = (bf16[4,8,2,32,128]{4,3,2,1,0:T(8,128)(2,1)S(1)}, bf16[4,8,2,32,128]{4,3,2,1,0:T(8,128)(2,1)S(1)}, u32[]{:S(2)}, u32[]{:S(2)}) collective-permute-start(bf16[4,8,2,32,128]{4,3,2,1,0:T(8,128)(2,1)S(1)} %get-tuple-element.27), channel_id=1, source_target_pairs={{0,8},{8,0},{1,9},{9,1},{2,10},{10,2},{3,11},{11,3},{4,12},{12,4},... | collective-permute-start | bytes 1572872 | tf_op jit(solution)/shard_map/ppermute | solution.py:308

commit v4 on v3

--- a/solution.py
+++ b/solution.py
@@ -18,7 +18,7 @@
 GRP = N_CC * N_Y
 ROWS = 32
 QB = 256
-RC = 64
+RC = 256
 VM = pltpu.VMEM
 
 
@@ -117,8 +117,8 @@
 
 
 def other_kernel(
-    doc_ref, all_ref, oth_ref, e_ref, w_ref, m_ref, l_ref,
-    out_ref, sent_ref, b_ref, d_ref, k_ref, v_oth, acc,
+    doc_ref, all_ref, oth_ref, e_ref, m_ref, l_ref,
+    out_ref, sent_ref, b_ref, d_ref, k_ref, f_ref, delta_ref, v_oth, acc,
 ):
     half, lead, slots = placed()
     for t in range(N_CC):
@@ -139,7 +139,10 @@
 
     def scores(u):
         n, r = QB * (u + 1), rows_of(u)
-        return dot_nt(all_ref[2, r], k_ref[:n]), dot_nt(all_ref[3, r], v_oth[:n])
+        return dot_nt(all_ref[2, r], k_ref[:n])
+
+    def weights(u):
+        return dot_nt(all_ref[3, rows_of(u)], v_oth[: QB * (u + 1)])
 
     def softmax(u, s):
         n = QB * (u + 1)
@@ -152,11 +155,13 @@
             e = jnp.exp2((piece - top) * (SCALE * LOG2E))
             fade = jnp.exp2((m_own - top) * (SCALE * LOG2E))
             inv = 1.0 / (l_ref[part, :1] * fade + jnp.sum(e, axis=1, keepdims=True))
-            p1, p2 = e_ref[part, :n] * (fade * inv), e * inv
-            parts.append((p1, p2, p1.astype(jnp.bfloat16), p2.astype(jnp.bfloat16)))
-        p1, p2, b1, b2 = joined(parts)
+            fade = fade * inv
+            f_ref[part] = jnp.broadcast_to(fade, (RC, HD))
+            b1, p2 = (e_ref[part, :n] * fade).astype(jnp.bfloat16), e * inv
+            parts.append((p2, b1, p2.astype(jnp.bfloat16)))
+        p2, b1, b2 = joined(parts)
         b_ref[rows_of(u), :n] = b1
-        return p1, p2, b1, b2
+        return p2, b1, b2
 
     def output(u, b1, b2):
         n = QB * (u + 1)
@@ -165,59 +170,64 @@
             out_ref[:, slots[2 * u + i]] = out[i * BLK : (i + 1) * BLK].reshape(N_Y, ROWS, HD)
         return out
 
-    def score_grads(u, p1, p2, w, out):
+    def score_grads(u, p2, w, out):
         n = QB * (u + 1)
         parts = []
         for low, part in chunks(u):
             some = slice(low, low + RC)
             g = all_ref[3, part].astype(jnp.float32)
             delta = jnp.sum(g * out[some].astype(jnp.float32), axis=1, keepdims=True)
-            d2 = (p2[some] * (w[some] - delta)).astype(jnp.bfloat16)
-            d_ref[0, part, :n] = (p1[some] * (w_ref[part, :n] - delta)).astype(jnp.bfloat16)
-            d_ref[1, part, :n] = d2
-            parts.append((d2,))
-        return joined(parts)[0]
-
-    def key_grads(u, d2, b2):
+            delta_ref[part] = jnp.broadcast_to(delta, (RC, HD))
+            parts.append(((p2[some] * (w[some] - delta)).astype(jnp.bfloat16),))
+        d2 = joined(parts)[0]
+        d_ref[rows_of(u), :n] = d2
+        return d2
+
+    def key_grads(u, a, right):
         n, r = QB * (u + 1), rows_of(u)
-        for a, left, right in ((0, all_ref[2, r].T, d2), (1, all_ref[3, r].T, b2)):
-            new = dot_nn(left, right)
-            if u < last:
-                new = acc[a, :, :n] + new
-            if u:
-                acc[a, :, : n - QB] = new[:, : n - QB]
-            done = (new[:, n - QB :] * (1.0 if a else SCALE)).astype(jnp.bfloat16).T
-            for i in range(2):
-                part = done[i * BLK : (i + 1) * BLK].reshape(N_Y, ROWS, HD)
-                sent_ref[:, slots[2 * u + i], a] = part
+        new = dot_nn(all_ref[2 + a, r].T, right)
+        if u < last:
+            new = acc[a, :, :n] + new
+        if u:
+            acc[a, :, : n - QB] = new[:, : n - QB]
+        done = (new[:, n - QB :] * (1.0 if a else SCALE)).astype(jnp.bfloat16).T
+        for i in range(2):
+            part = done[i * BLK : (i + 1) * BLK].reshape(N_Y, ROWS, HD)
+            sent_ref[:, slots[2 * u + i], a] = part
 
     ready = scores(last)
-    before = None
-    for u in reversed(range(-1, last + 1)):
-        s, w = ready
-        if u > 0:
+    kept = {}
+    for u in reversed(range(last + 1)):
+        s = ready
+        if u:
             ready = scores(u - 1)
-        if before is not None:
-            p1, p2, b2, w_b, out = before
-            d2 = score_grads(u + 1, p1, p2, w_b, out)
-        if u >= 0:
-            q1, q2, c1, c2 = softmax(u, s)
-        if before is not None:
-            key_grads(u + 1, d2, b2)
-        if u >= 0:
-            before = q1, q2, c2, w, output(u, c1, c2)
-
-
-def rest_kernel(all_ref, k_ref, b_ref, d_ref, dq_ref, own_ref):
+        p2, b1, b2 = softmax(u, s)
+        kept[u] = p2, output(u, b1, b2)
+        key_grads(u, 1, b2)
+    ready = weights(last)
+    for u in reversed(range(last + 1)):
+        w = ready
+        if u:
+            ready = weights(u - 1)
+        p2, out = kept[u]
+        key_grads(u, 0, score_grads(u, p2, w, out))
+
+
+def rest_kernel(
+    all_ref, k_ref, e_ref, w_ref, f_ref, delta_ref, b_ref, d_ref, dq_ref, own_ref, d_own
+):
     _, _, slots = placed()
     q_t, g_t = all_ref[2].T, all_ref[3].T
     for u in reversed(range(N_CC // 2)):
         n, r = QB * (u + 1), rows_of(u)
-        dq = dot_nn(d_ref[0, r, :n], all_ref[0, :n]) + dot_nn(d_ref[1, r, :n], k_ref[:n])
+        low = u * QB
+        dv = dot_nn(g_t[:, low:], b_ref[low:, r])
+        d = e_ref[r, :n] * f_ref[r, :1] * (w_ref[r, :n] - delta_ref[r, :1])
+        d = d.astype(jnp.bfloat16)
+        d_own[r, :n] = d
+        dq = dot_nn(d_ref[r, :n], k_ref[:n]) + dot_nn(d, all_ref[0, :n])
         dq = (dq * SCALE).astype(jnp.bfloat16)
-        low = u * QB
-        dk = dot_nn(q_t[:, low:], d_ref[0, low:, r]) * SCALE
-        dv = dot_nn(g_t[:, low:], b_ref[low:, r])
+        dk = dot_nn(q_t[:, low:], d_own[low:, r]) * SCALE
         for i in range(2):
             at, part = slots[2 * u + i], slice(i * BLK, (i + 1) * BLK)
             dq_ref[:, at] = dq[part].reshape(N_Y, ROWS, HD)
@@ -290,7 +300,7 @@
         in_specs=[smem, whole()],
         out_specs=(whole(),) * 5,
     )(block_doc, held(mine))
-    out, sent, probs, grads, k_other = pl.pallas_call(
+    out, sent, probs, grads, k_other, fade, delta = pl.pallas_call(
         other_kernel,
         name="other_keys",
         compiler_params=grant(24),
@@ -298,22 +308,25 @@
             near(N_Y, N_CC, ROWS, HD),
             near(N_Y, N_CC, 2, ROWS, HD),
             near(full, full),
-            near(2, full, full),
+            near(full, full),
             near(full, HD),
+            near(full, HD, kind=f32),
+            near(full, HD, kind=f32),
         ),
-        in_specs=[smem] + [whole()] * 6,
-        out_specs=(whole(),) * 5,
+        in_specs=[smem] + [whole()] * 5,
+        out_specs=(whole(),) * 7,
         scratch_shapes=[VM((full, HD), jnp.bfloat16), VM((2, HD, full), f32)],
-    )(block_doc, *[held(x) for x in (everything, other, exps, weights, top, total)])
+    )(block_doc, *[held(x) for x in (everything, other, exps, top, total)])
     received = lax.ppermute(sent, "core", swap)
     dq, own = pl.pallas_call(
         rest_kernel,
         name="rest",
         compiler_params=grant(16),
         out_shape=(near(N_Y, N_CC, ROWS, HD), near(N_Y, N_CC, 2, ROWS, HD, kind=f32)),
-        in_specs=[whole()] * 4,
+        in_specs=[whole()] * 8,
         out_specs=(whole(),) * 2,
-    )(*[held(x) for x in (everything, k_other, probs, grads)])
+        scratch_shapes=[VM((full, full), jnp.bfloat16)],
+    )(*[held(x) for x in (everything, k_other, exps, weights, fade, delta, probs, grads)])
     back = pl.pallas_call(
         combine_kernel,
         name="combine",

time: 59.3 us -> 58.5 us (0.987)
    pallas_call x1, Pallas kernels: 4.89 us -> 4.07 us  [per_device(): pl.pallas_call(other_kernel, name='other_keys', compiler_params=grant(24)...]
where the time goes in v4:
time: 58.5 us; the launch traced here: 58.3 us
  blocking collectives  47 us (80%)
  Pallas kernels  9.76 us (17%)
  between operations  0.7 us (1%)
    all_to_all x1, blocking collectives, per_device(): mine = lax.all_to_all(packed, ('y', 'cc'), 0, 0, tiled=True)  25.5 us
    all_to_all x1, blocking collectives, per_device(): lax.all_to_all(back.reshape(GRP, 4, ROWS, HD), ('y', 'cc'), 0, 0, tiled=T...  21.5 us
    pallas_call x1, Pallas kernels, per_device(): pl.pallas_call(other_kernel, name='other_keys', compiler_params=grant(24)...  4.07 us
    pallas_call x1, Pallas kernels, per_device(): pl.pallas_call(own_kernel, name='own_keys', compiler_params=grant(16), ou...  1.66 us
    pallas_call x1, Pallas kernels, per_device(): pl.pallas_call(rest_kernel, name='rest', compiler_params=grant(16), out_s...  1.53 us
    pallas_call x1, Pallas kernels, per_device(): pl.pallas_call(pack_kernel, name='pack', compiler_params=grant(8), out_sh...  1.27 us
  transfers between devices with their start and end apart: 2, of which 2 were waited for; matrix products, arithmetic and copies ran while one was open for 0% of the time, Pallas kernels for 5%

profile of v4, /device:TPU:0, one launch (start us, length us, event | category | flops | bytes accessed | tf_op | source)
XLA Modules:
  0.0 58.3 jit_solution(803060848102337230)
XLA Ops:
  0.6 0.0 copy-start
  0.6 1.3 %pack.1 = bf16[32,4,32,128]{3,2,1,0:T(8,128)(2,1)S(1)} custom-call(bf16[32,4096]{1,0:T(8,128)(2,1)} %k_ref.1, bf16[32,4096]{1,0:T(8,128)(2,1)} %v_ref.1, bf16[32,4096]{1,0:T(8,128)(2,1)} %q_ref.1, bf16[32,4096]{1,0:T(8,128)(2,1)} %g_ref.1), custom_call_target="tpu_custom_call" | custom-call | tf_op jit(solution)/shard_map/pack/pallas_call | solution.py:273
  1.9 25.5 %all_to_all.10 = bf16[32,4,32,128]{3,2,1,0:T(8,128)(2,1)S(1)} all-to-all(bf16[32,4,32,128]{3,2,1,0:T(8,128)(2,1)S(1)} %pack.1), channel_id=1, replica_groups=mesh['cc'=8,'core'=2,'xh'=2,'y'=4] {'y','cc'}, dimensions={0} | all-to-all | bytes 2097152 | tf_op jit(solution)/shard_map/all_to_all | solution.py:282
  27.5 0.1 collective-permute-start
  27.6 0.0 copy-done
  27.6 1.7 %own_keys.1 = (bf16[4,1024,128]{2,1,0:T(8,128)(2,1)S(1)}, f32[1024,1024]{1,0:T(8,128)S(1)}, f32[1024,1024]{1,0:T(8,128)S(1)}, f32[1024,128]{1,0:T(8,128)S(1)}, f32[1024,128]{1,0:T(8,128)S(1)}) custom-call(s32[32]{0:T(128)S(1)} %copy-done, bf16[4,8,4,32,128]{4,3,2,1,0:T(8,128)(2,1)S(1)} %bitcast.3), custom_call_target="tpu_custom_call" | custom-call | tf_op jit(solution)/shard_map/own_keys/pallas_call | solution.py:289
  29.3 0.2 collective-permute-done.oth_ref
  29.5 4.1 %other_keys.1 = (bf16[4,8,32,128]{3,2,1,0:T(8,128)(2,1)S(1)}, bf16[4,8,2,32,128]{4,3,2,1,0:T(8,128)(2,1)S(1)}, bf16[1024,1024]{1,0:T(8,128)(2,1)S(1)}, bf16[1024...) custom-call(s32[32]{0:T(128)S(1)} %copy-done, ...), custom_call_target="tpu_custom_call" | custom-call | tf_op jit(solution)/shard_map/other_keys/pallas_call | solution.py:303
  33.6 0.4 collective-permute-start.1
  34.0 1.5 %rest.1 = (bf16[4,8,32,128]{3,2,1,0:T(8,128)(2,1)S(1)}, f32[4,8,2,32,128]{4,3,2,1,0:T(8,128)S(1)}) custom-call(bf16[4,1024,128]{2,1,0:T(8,128)(2,1)S(1)} %get-tuple-element.18.all_ref, bf16[1024,128]{1,0:T(8,128)(2,1)S(1)} %get-tuple-element.23.k_ref, f32[1024,1024]{1,0:T(8,128)S(1)} %get-tuple-element.19.e_ref, f32[1024,1024]{1,0:T(8,128)S(1)} %get-tuple-element.24.w_ref, ...), custom_call_target="tpu_custom_call" | custom-call | tf_op jit(solution)/shard_map/rest/pallas_call | solution.py:321
  35.5 0.1 collective-permute-done.1.recv_ref
  35.6 0.2 combine.1
  35.8 21.5 %all_to_all.11.x_ref = bf16[32,4,32,128]{3,2,1,0:T(8,128)(2,1)S(1)} all-to-all(bf16[32,4,32,128]{3,2,1,0:T(8,128)(2,1)S(1)} %bitcast.4), channel_id=1, replica_groups=mesh['cc'=8,'core'=2,'xh'=2,'y'=4] {'y','cc'}, dimensions={0} | all-to-all | bytes 2097152 | tf_op jit(solution)/shard_map/all_to_all | solution.py:338
  57.3 1.0 %unpack.1 = (bf16[32,4096]{1,0:T(8,128)(2,1)}, bf16[32,4096]{1,0:T(8,128)(2,1)}, bf16[32,4096]{1,0:T(8,128)(2,1)}, bf16[32,4096]{1,0:T(8,128)(2,1)}) custom-call(bf16[32,4,32,128]{3,2,1,0:T(8,128)(2,1)S(1)} %all_to_all.11.x_ref), custom_call_target="tpu_custom_call" | custom-call | tf_op jit(solution)/shard_map/unpack/pallas_call | solution.py:340
  (1 shorter events, 0.0 us)
Async XLA Ops:
  0.6 27.0 %copy-start = (s32[32]{0:T(128)S(1)}, s32[32]{0:T(128)}, u32[]{:S(2)}) copy-start(s32[32]{0:T(128)} %doc_ref.3) | copy-start | bytes 388
  27.5 2.0 %collective-permute-start = (bf16[4,8,2,32,128]{4,3,2,1,0:T(8,128)(2,1)S(1)}, bf16[4,8,2,32,128]{4,3,2,1,0:T(8,128)(2,1)S(1)}, u32[]{:S(2)}, u32[]{:S(2)}) collective-permute-start(bf16[4,8,2,32,128]{4,3,2,1,0:T(8,128)(2,1)S(1)} %slice.4), channel_id=1, source_target_pairs={{0,8},{8,0},{1,9},{9,1},{2,10},{10,2},{3,11},{11,3},{4,12},{12,4},... | collective-permute-start | bytes 1572872 | tf_op jit(solution)/shard_map/ppermute | solution.py:285
  33.6 2.0 %collective-permute-start.1 = (bf16[4,8,2,32,128]{4,3,2,1,0:T(8,128)(2,1)S(1)}, bf16[4,8,2,32,128]{4,3,2,1,0:T(8,128)(2,1)S(1)}, u32[]{:S(2)}, u32[]{:S(2)}) collective-permute-start(bf16[4,8,2,32,128]{4,3,2,1,0:T(8,128)(2,1)S(1)} %get-tuple-element.31), channel_id=1, source_target_pairs={{0,8},{8,0},{1,9},{9,1},{2,10},{10,2},{3,11},{11,3},{4,12},{12,4},... | collective-permute-start | bytes 1572872 | tf_op jit(solution)/shard_map/ppermute | solution.py:320

commit v5 on v4

--- a/solution.py
+++ b/solution.py
@@ -22,13 +22,32 @@
 VM = pltpu.VMEM
 
 
-def pack_kernel(k_ref, v_ref, q_ref, g_ref, o_ref, buf, sems):
+def write_bias(doc, bias_ref):
+    half, lead, _ = placed()
+    own = [doc[half * 16 + 2 * t + lead] for t in range(N_CC)]
+    other = [doc[half * 16 + 2 * t + 1 - lead] for t in range(N_CC)]
+    for t in range(N_CC):
+        for tk in range(t + 1):
+            at = slice(tk * BLK, (tk + 1) * BLK)
+            for a, keys in enumerate((own, other)):
+                hidden = keys[tk] != own[t]
+                if a and tk == t:
+                    hidden = hidden | (lead == 0)
+                value = jnp.where(hidden, NEG, 0.0)
+                bias_ref[a, t : t + 1, at] = jnp.full((1, BLK), value, jnp.float32)
+
+
+def pack_kernel(doc_ref, k_ref, v_ref, q_ref, g_ref, o_ref, bias_ref, buf, sems, doc, doc_sem):
+    doc_copy = pltpu.make_async_copy(doc_ref, doc, doc_sem)
+    doc_copy.start()
     copies = [
         pltpu.make_async_copy(ref, buf.at[a], sems.at[a])
         for a, ref in enumerate((k_ref, v_ref, q_ref, g_ref))
     ]
     for copy in copies:
         copy.start()
+    doc_copy.wait()
+    write_bias(doc, bias_ref)
     for a, copy in enumerate(copies):
         copy.wait()
         for h in range(GRP):
@@ -86,12 +105,11 @@
     return [jnp.concatenate(column, axis=0) for column in zip(*parts)]
 
 
-def own_kernel(doc_ref, x_ref, all_ref, e_ref, w_ref, m_ref, l_ref):
-    half, lead, slots = placed()
+def own_kernel(bias_ref, x_ref, all_ref, e_ref, w_ref, m_ref, l_ref, o_ref):
+    _, _, slots = placed()
     for t in range(N_CC):
         for a in range(4):
             all_ref[a, t * BLK : (t + 1) * BLK] = x_ref[:, slots[t], a].reshape(BLK, HD)
-    doc = [doc_ref[half * 16 + 2 * t + lead] for t in range(N_CC)]
     below = lax.broadcasted_iota(jnp.int32, (BLK, BLK), 1) <= lax.broadcasted_iota(
         jnp.int32, (BLK, BLK), 0
     )
@@ -101,39 +119,41 @@
             return jnp.full_like(tile, NEG)
         if tk == t:
             return jnp.where(below, tile, NEG)
-        return tile + jnp.where(doc[tk] == doc[t], 0.0, NEG)
-
-    for u in reversed(range(N_CC // 2)):
+        return tile + bias_ref[0, t : t + 1, tk * BLK : (tk + 1) * BLK]
+
+    last = N_CC // 2 - 1
+
+    def scores(u):
+        return dot_nt(all_ref[2, rows_of(u)], all_ref[0, : QB * (u + 1)])
+
+    ready = scores(last)
+    for u in reversed(range(last + 1)):
         n, r = QB * (u + 1), rows_of(u)
-        s = masked(dot_nt(all_ref[2, r], all_ref[0, :n]), u, bias)
+        s = masked(ready, u, bias)
+        if u:
+            ready = scores(u - 1)
         w_ref[r, :n] = dot_nt(all_ref[3, r], all_ref[1, :n])
-        for low, part in chunks(u):
-            piece = s[low : low + RC]
-            top = jnp.max(piece, axis=1, keepdims=True)
-            e = jnp.exp2((piece - top) * (SCALE * LOG2E))
-            e_ref[part, :n] = e
-            m_ref[part] = jnp.broadcast_to(top, (RC, HD))
-            l_ref[part] = jnp.broadcast_to(jnp.sum(e, axis=1, keepdims=True), (RC, HD))
+        top = jnp.max(s, axis=1, keepdims=True)
+        e = jnp.exp2((s - top) * (SCALE * LOG2E))
+        e_ref[r, :n] = e
+        m_ref[r] = jnp.broadcast_to(top, (QB, HD))
+        l_ref[r] = jnp.broadcast_to(jnp.sum(e, axis=1, keepdims=True), (QB, HD))
+        o_ref[r] = dot_nn(e.astype(jnp.bfloat16), all_ref[1, :n])
 
 
 def other_kernel(
-    doc_ref, all_ref, oth_ref, e_ref, m_ref, l_ref,
-    out_ref, sent_ref, b_ref, d_ref, k_ref, f_ref, delta_ref, v_oth, acc,
+    bias_ref, all_ref, oth_ref, o_ref, m_ref, l_ref,
+    out_ref, sent_ref, d_ref, k_ref, f_ref, delta_ref, v_oth, acc,
 ):
-    half, lead, slots = placed()
+    _, _, slots = placed()
     for t in range(N_CC):
         k_ref[t * BLK : (t + 1) * BLK] = oth_ref[:, slots[t], 0].reshape(BLK, HD)
         v_oth[t * BLK : (t + 1) * BLK] = oth_ref[:, slots[t], 1].reshape(BLK, HD)
-    doc_own = [doc_ref[half * 16 + 2 * t + lead] for t in range(N_CC)]
-    doc_oth = [doc_ref[half * 16 + 2 * t + 1 - lead] for t in range(N_CC)]
 
     def bias(t, tk, tile):
         if tk > t:
             return jnp.full_like(tile, NEG)
-        seen = doc_oth[tk] == doc_own[t]
-        if tk == t:
-            seen = seen & (lead == 1)
-        return tile + jnp.where(seen, 0.0, NEG)
+        return tile + bias_ref[1, t : t + 1, tk * BLK : (tk + 1) * BLK]
 
     last = N_CC // 2 - 1
 
@@ -157,15 +177,12 @@
             inv = 1.0 / (l_ref[part, :1] * fade + jnp.sum(e, axis=1, keepdims=True))
             fade = fade * inv
             f_ref[part] = jnp.broadcast_to(fade, (RC, HD))
-            b1, p2 = (e_ref[part, :n] * fade).astype(jnp.bfloat16), e * inv
-            parts.append((p2, b1, p2.astype(jnp.bfloat16)))
-        p2, b1, b2 = joined(parts)
-        b_ref[rows_of(u), :n] = b1
-        return p2, b1, b2
-
-    def output(u, b1, b2):
-        n = QB * (u + 1)
-        out = (dot_nn(b1, all_ref[1, :n]) + dot_nn(b2, v_oth[:n])).astype(jnp.bfloat16)
+            p2 = e * inv
+            parts.append((p2, p2.astype(jnp.bfloat16), o_ref[part] * fade))
+        return joined(parts)
+
+    def output(u, b2, own):
+        out = (own + dot_nn(b2, v_oth[: QB * (u + 1)])).astype(jnp.bfloat16)
         for i in range(2):
             out_ref[:, slots[2 * u + i]] = out[i * BLK : (i + 1) * BLK].reshape(N_Y, ROWS, HD)
         return out
@@ -201,8 +218,8 @@
         s = ready
         if u:
             ready = scores(u - 1)
-        p2, b1, b2 = softmax(u, s)
-        kept[u] = p2, output(u, b1, b2)
+        p2, b2, own = softmax(u, s)
+        kept[u] = p2, output(u, b2, own)
         key_grads(u, 1, b2)
     ready = weights(last)
     for u in reversed(range(last + 1)):
@@ -214,16 +231,17 @@
 
 
 def rest_kernel(
-    all_ref, k_ref, e_ref, w_ref, f_ref, delta_ref, b_ref, d_ref, dq_ref, own_ref, d_own
+    all_ref, k_ref, e_ref, w_ref, f_ref, delta_ref, d_ref, dq_ref, own_ref, b_own, d_own
 ):
     _, _, slots = placed()
     q_t, g_t = all_ref[2].T, all_ref[3].T
     for u in reversed(range(N_CC // 2)):
         n, r = QB * (u + 1), rows_of(u)
         low = u * QB
-        dv = dot_nn(g_t[:, low:], b_ref[low:, r])
-        d = e_ref[r, :n] * f_ref[r, :1] * (w_ref[r, :n] - delta_ref[r, :1])
-        d = d.astype(jnp.bfloat16)
+        p = e_ref[r, :n] * f_ref[r, :1]
+        b_own[r, :n] = p.astype(jnp.bfloat16)
+        dv = dot_nn(g_t[:, low:], b_own[low:, r])
+        d = (p * (w_ref[r, :n] - delta_ref[r, :1])).astype(jnp.bfloat16)
         d_own[r, :n] = d
         dq = dot_nn(d_ref[r, :n], k_ref[:n]) + dot_nn(d, all_ref[0, :n])
         dq = (dq * SCALE).astype(jnp.bfloat16)
@@ -270,23 +288,24 @@
 
 
 def per_device(queries, keys, values, grad_out, block_doc):
-    packed = pl.pallas_call(
+    full = N_CC * BLK
+    packed, hide = pl.pallas_call(
         pack_kernel,
         name="pack",
         compiler_params=grant(8),
-        out_shape=near(GRP, 4, ROWS, HD),
-        in_specs=[whole(pltpu.HBM)] * 4,
-        out_specs=whole(),
-        scratch_shapes=staging(),
-    )(*[far(x) for x in (keys, values, queries, grad_out)])
+        out_shape=(near(GRP, 4, ROWS, HD), near(2, N_CC, full, kind=jnp.float32)),
+        in_specs=[whole(pltpu.HBM)] * 5,
+        out_specs=(whole(), whole()),
+        scratch_shapes=staging()
+        + [pltpu.SMEM(block_doc.shape, jnp.int32), pltpu.SemaphoreType.DMA],
+    )(*[far(x) for x in (block_doc, keys, values, queries, grad_out)])
+    hide = held(hide)
     mine = lax.all_to_all(packed, ("y", "cc"), 0, 0, tiled=True)
     swap = [(0, 1), (1, 0)]
     mine = mine.reshape(N_Y, N_CC, 4, ROWS, HD)
     other = lax.ppermute(mine[:, :, 0:2], "core", swap)
-    smem = whole(pltpu.SMEM)
-    full = N_CC * BLK
     f32 = jnp.float32
-    everything, exps, weights, top, total = pl.pallas_call(
+    everything, exps, weights, top, total, partial = pl.pallas_call(
         own_kernel,
         name="own_keys",
         compiler_params=grant(16),
@@ -296,11 +315,12 @@
             near(full, full, kind=f32),
             near(full, HD, kind=f32),
             near(full, HD, kind=f32),
+            near(full, HD, kind=f32),
         ),
-        in_specs=[smem, whole()],
-        out_specs=(whole(),) * 5,
-    )(block_doc, held(mine))
-    out, sent, probs, grads, k_other, fade, delta = pl.pallas_call(
+        in_specs=[whole()] * 2,
+        out_specs=(whole(),) * 6,
+    )(hide, held(mine))
+    out, sent, grads, k_other, fade, delta = pl.pallas_call(
         other_kernel,
         name="other_keys",
         compiler_params=grant(24),
@@ -308,25 +328,24 @@
             near(N_Y, N_CC, ROWS, HD),
             near(N_Y, N_CC, 2, ROWS, HD),
             near(full, full),
-            near(full, full),
             near(full, HD),
             near(full, HD, kind=f32),
             near(full, HD, kind=f32),
         ),
-        in_specs=[smem] + [whole()] * 5,
-        out_specs=(whole(),) * 7,
+        in_specs=[whole()] * 6,
+        out_specs=(whole(),) * 6,
         scratch_shapes=[VM((full, HD), jnp.bfloat16), VM((2, HD, full), f32)],
-    )(block_doc, *[held(x) for x in (everything, other, exps, top, total)])
+    )(hide, *[held(x) for x in (everything, other, partial, top, total)])
     received = lax.ppermute(sent, "core", swap)
     dq, own = pl.pallas_call(
         rest_kernel,
         name="rest",
         compiler_params=grant(16),
         out_shape=(near(N_Y, N_CC, ROWS, HD), near(N_Y, N_CC, 2, ROWS, HD, kind=f32)),
-        in_specs=[whole()] * 8,
+        in_specs=[whole()] * 7,
         out_specs=(whole(),) * 2,
-        scratch_shapes=[VM((full, full), jnp.bfloat16)],
-    )(*[held(x) for x in (everything, k_other, exps, weights, fade, delta, probs, grads)])
+        scratch_shapes=[VM((full, full), jnp.bfloat16)] * 2,
+    )(*[held(x) for x in (everything, k_other, exps, weights, fade, delta, grads)])
     back = pl.pallas_call(
         combine_kernel,
         name="combine",

time: 58.5 us -> 57.5 us (0.983)
  Pallas kernels: 9.76 us -> 8.59 us
    pallas_call x1, Pallas kernels: 4.07 us -> 3.31 us  [per_device(): pl.pallas_call(other_kernel, name='other_keys', compiler_params=grant(24)...]
where the time goes in v5:
time: 57.5 us; the launch traced here: 57.3 us
  blocking collectives  46.9 us (82%)
  Pallas kernels  8.59 us (15%)
  waiting for transfers between devices  0.83 us (1%)
  between operations  0.68 us (1%)
    all_to_all x1, blocking collectives, per_device(): mine = lax.all_to_all(packed, ('y', 'cc'), 0, 0, tiled=True)  25.5 us
    all_to_all x1, blocking collectives, per_device(): lax.all_to_all(back.reshape(GRP, 4, ROWS, HD), ('y', 'cc'), 0, 0, tiled=T...  21.3 us
    pallas_call x1, Pallas kernels, per_device(): pl.pallas_call(other_kernel, name='other_keys', compiler_params=grant(24)...  3.31 us
    pallas_call x1, Pallas kernels, per_device(): pl.pallas_call(rest_kernel, name='rest', compiler_params=grant(16), out_s...  1.47 us
    pallas_call x1, Pallas kernels, per_device(): pl.pallas_call(own_kernel, name='own_keys', compiler_params=grant(16), ou...  1.38 us
    pallas_call x1, Pallas kernels, per_device(): pl.pallas_call(pack_kernel, name='pack', compiler_params=grant(8), out_sh...  1.28 us
  transfers between devices with their start and end apart: 2, of which 2 were waited for; matrix products, arithmetic and copies ran while one was open for 0% of the time, Pallas kernels for 5%

profile of v5, /device:TPU:0, one launch (start us, length us, event | category | flops | bytes accessed | tf_op | source)
XLA Modules:
  0.0 57.3 jit_solution(11891162513921052247)
XLA Ops:
  0.6 1.3 %pack.1 = (bf16[32,4,32,128]{3,2,1,0:T(8,128)(2,1)S(1)}, f32[2,8,1024]{2,1,0:T(8,128)S(1)}) custom-call(s32[32]{0:T(128)} %doc_ref.1, bf16[32,4096]{1,0:T(8,128)(2,1)} %k_ref.1, bf16[32,4096]{1,0:T(8,128)(2,1)} %v_ref.1, bf16[32,4096]{1,0:T(8,128)(2,1)} %q_ref.1, bf16[32,4096]{1,0:T(8,128)(2,1)} %g_ref.1), custom_call_target="tpu_custom_call" | custom-call | tf_op jit(solution)/shard_map/pack/pallas_call | solution.py:292
  1.9 25.5 %all_to_all.10 = bf16[32,4,32,128]{3,2,1,0:T(8,128)(2,1)S(1)} all-to-all(bf16[32,4,32,128]{3,2,1,0:T(8,128)(2,1)S(1)} %get-tuple-element.21), channel_id=1, replica_groups=mesh['cc'=8,'core'=2,'xh'=2,'y'=4] {'y','cc'}, dimensions={0} | all-to-all | bytes 2097152 | tf_op jit(solution)/shard_map/all_to_all | solution.py:303
  27.5 0.1 collective-permute-start
  27.6 1.4 %own_keys.1 = (bf16[4,1024,128]{2,1,0:T(8,128)(2,1)S(1)}, f32[1024,1024]{1,0:T(8,128)S(1)}, f32[1024,1024]{1,0:T(8,128)S(1)}, f32[1024,128]{1,0:T(8,128)S(1)}, f...) custom-call(f32[2,8,1024]{2,1,0:T(8,128)S(1)} %get-tuple-element.20.bias_ref, bf16[4,8,4,32,128]{4,3,2,1,0:T(8,128)(2,1)S(1)} %bitcast.3), custom_call_target="tpu_custom_call" | custom-call | tf_op jit(solution)/shard_map/own_keys/pallas_call | solution.py:308
  29.0 0.5 collective-permute-done.oth_ref
  29.5 3.3 %other_keys.1 = (bf16[4,8,32,128]{3,2,1,0:T(8,128)(2,1)S(1)}, bf16[4,8,2,32,128]{4,3,2,1,0:T(8,128)(2,1)S(1)}, bf16[1024,1024]{1,0:T(8,128)(2,1)S(1)}, bf16[1024...) custom-call(f32[2,8,1024]{2,1,0:T(8,128)S(1)} %get-tuple-element.20.bias_ref, ...), custom_call_target="tpu_custom_call" | custom-call | tf_op jit(solution)/shard_map/other_keys/pallas_call | solution.py:323
  32.8 0.2 collective-permute-start.1
  33.0 1.5 %rest.1 = (bf16[4,8,32,128]{3,2,1,0:T(8,128)(2,1)S(1)}, f32[4,8,2,32,128]{4,3,2,1,0:T(8,128)S(1)}) custom-call(bf16[4,1024,128]{2,1,0:T(8,128)(2,1)S(1)} %get-tuple-element.22.all_ref, bf16[1024,128]{1,0:T(8,128)(2,1)S(1)} %get-tuple-element.27.k_ref, f32[1024,1024]{1,0:T(8,128)S(1)} %get-tuple-element.28.e_ref, f32[1024,1024]{1,0:T(8,128)S(1)} %get-tuple-element.29.w_ref, ...), custom_call_target="tpu_custom_call" | custom-call | tf_op jit(solution)/shard_map/rest/pallas_call | solution.py:340
  34.5 0.3 collective-permute-done.1.recv_ref
  34.8 0.1 combine.1
  34.9 21.3 %all_to_all.11.x_ref = bf16[32,4,32,128]{3,2,1,0:T(8,128)(2,1)S(1)} all-to-all(bf16[32,4,32,128]{3,2,1,0:T(8,128)(2,1)S(1)} %bitcast.4), channel_id=1, replica_groups=mesh['cc'=8,'core'=2,'xh'=2,'y'=4] {'y','cc'}, dimensions={0} | all-to-all | bytes 2097152 | tf_op jit(solution)/shard_map/all_to_all | solution.py:357
  56.3 1.0 %unpack.1 = (bf16[32,4096]{1,0:T(8,128)(2,1)}, bf16[32,4096]{1,0:T(8,128)(2,1)}, bf16[32,4096]{1,0:T(8,128)(2,1)}, bf16[32,4096]{1,0:T(8,128)(2,1)}) custom-call(bf16[32,4,32,128]{3,2,1,0:T(8,128)(2,1)S(1)} %all_to_all.11.x_ref), custom_call_target="tpu_custom_call" | custom-call | tf_op jit(solution)/shard_map/unpack/pallas_call | solution.py:359
  (1 shorter events, 0.0 us)
Async XLA Ops:
  27.5 2.0 %collective-permute-start = (bf16[4,8,2,32,128]{4,3,2,1,0:T(8,128)(2,1)S(1)}, bf16[4,8,2,32,128]{4,3,2,1,0:T(8,128)(2,1)S(1)}, u32[]{:S(2)}, u32[]{:S(2)}) collective-permute-start(bf16[4,8,2,32,128]{4,3,2,1,0:T(8,128)(2,1)S(1)} %slice.4), channel_id=1, source_target_pairs={{0,8},{8,0},{1,9},{9,1},{2,10},{10,2},{3,11},{11,3},{4,12},{12,4},... | collective-permute-start | bytes 1572872 | tf_op jit(solution)/shard_map/ppermute | solution.py:306
  32.8 2.0 %collective-permute-start.1 = (bf16[4,8,2,32,128]{4,3,2,1,0:T(8,128)(2,1)S(1)}, bf16[4,8,2,32,128]{4,3,2,1,0:T(8,128)(2,1)S(1)}, u32[]{:S(2)}, u32[]{:S(2)}) collective-permute-start(bf16[4,8,2,32,128]{4,3,2,1,0:T(8,128)(2,1)S(1)} %get-tuple-element.35), channel_id=1, source_target_pairs={{0,8},{8,0},{1,9},{9,1},{2,10},{10,2},{3,11},{11,3},{4,12},{12,4},... | collective-permute-start | bytes 1572872 | tf_op jit(solution)/shard_map/ppermute | solution.py:339

commit v6 on v5

--- a/solution.py
+++ b/solution.py
@@ -212,22 +212,23 @@
             part = done[i * BLK : (i + 1) * BLK].reshape(N_Y, ROWS, HD)
             sent_ref[:, slots[2 * u + i], a] = part
 
-    ready = scores(last)
+    ready = scores(0)
     kept = {}
-    for u in reversed(range(last + 1)):
+    for u in range(last + 1):
         s = ready
-        if u:
-            ready = scores(u - 1)
+        if u < last:
+            ready = scores(u + 1)
         p2, b2, own = softmax(u, s)
-        kept[u] = p2, output(u, b2, own)
-        key_grads(u, 1, b2)
+        kept[u] = p2, b2, output(u, b2, own)
     ready = weights(last)
     for u in reversed(range(last + 1)):
         w = ready
         if u:
             ready = weights(u - 1)
-        p2, out = kept[u]
-        key_grads(u, 0, score_grads(u, p2, w, out))
+        p2, b2, out = kept[u]
+        d2 = score_grads(u, p2, w, out)
+        key_grads(u, 1, b2)
+        key_grads(u, 0, d2)
 
 
 def rest_kernel(

time: 57.5 us -> 57.3 us (level)
  no operation moved by 1% of the time
where the time goes in v6:
time: 57.3 us; the launch traced here: 57.1 us
  blocking collectives  46.9 us (82%)
  Pallas kernels  8.37 us (15%)
  waiting for transfers between devices  0.83 us (1%)
  between operations  0.68 us (1%)
    all_to_all x1, blocking collectives, per_device(): mine = lax.all_to_all(packed, ('y', 'cc'), 0, 0, tiled=True)  25.5 us
    all_to_all x1, blocking collectives, per_device(): lax.all_to_all(back.reshape(GRP, 4, ROWS, HD), ('y', 'cc'), 0, 0, tiled=T...  21.3 us
    pallas_call x1, Pallas kernels, per_device(): pl.pallas_call(other_kernel, name='other_keys', compiler_params=grant(24)...  3.09 us
    pallas_call x1, Pallas kernels, per_device(): pl.pallas_call(rest_kernel, name='rest', compiler_params=grant(16), out_s...  1.47 us
    pallas_call x1, Pallas kernels, per_device(): pl.pallas_call(own_kernel, name='own_keys', compiler_params=grant(16), ou...  1.38 us
    pallas_call x1, Pallas kernels, per_device(): pl.pallas_call(pack_kernel, name='pack', compiler_params=grant(8), out_sh...  1.28 us
  transfers between devices with their start and end apart: 2, of which 2 were waited for; matrix products, arithmetic and copies ran while one was open for 0% of the time, Pallas kernels for 5%

profile of v6, /device:TPU:0, one launch (start us, length us, event | category | flops | bytes accessed | tf_op | source)
XLA Modules:
  0.0 57.1 jit_solution(11558241413466786214)
XLA Ops:
  0.6 1.3 %pack.1 = (bf16[32,4,32,128]{3,2,1,0:T(8,128)(2,1)S(1)}, f32[2,8,1024]{2,1,0:T(8,128)S(1)}) custom-call(s32[32]{0:T(128)} %doc_ref.1, bf16[32,4096]{1,0:T(8,128)(2,1)} %k_ref.1, bf16[32,4096]{1,0:T(8,128)(2,1)} %v_ref.1, bf16[32,4096]{1,0:T(8,128)(2,1)} %q_ref.1, bf16[32,4096]{1,0:T(8,128)(2,1)} %g_ref.1), custom_call_target="tpu_custom_call" | custom-call | tf_op jit(solution)/shard_map/pack/pallas_call | solution.py:293
  1.9 25.5 %all_to_all.10 = bf16[32,4,32,128]{3,2,1,0:T(8,128)(2,1)S(1)} all-to-all(bf16[32,4,32,128]{3,2,1,0:T(8,128)(2,1)S(1)} %get-tuple-element.21), channel_id=1, replica_groups=mesh['cc'=8,'core'=2,'xh'=2,'y'=4] {'y','cc'}, dimensions={0} | all-to-all | bytes 2097152 | tf_op jit(solution)/shard_map/all_to_all | solution.py:304
  27.5 0.1 collective-permute-start
  27.6 1.4 %own_keys.1 = (bf16[4,1024,128]{2,1,0:T(8,128)(2,1)S(1)}, f32[1024,1024]{1,0:T(8,128)S(1)}, f32[1024,1024]{1,0:T(8,128)S(1)}, f32[1024,128]{1,0:T(8,128)S(1)}, f...) custom-call(f32[2,8,1024]{2,1,0:T(8,128)S(1)} %get-tuple-element.20.bias_ref, bf16[4,8,4,32,128]{4,3,2,1,0:T(8,128)(2,1)S(1)} %bitcast.3), custom_call_target="tpu_custom_call" | custom-call | tf_op jit(solution)/shard_map/own_keys/pallas_call | solution.py:309
  29.0 0.5 collective-permute-done.oth_ref
  29.5 3.1 %other_keys.1 = (bf16[4,8,32,128]{3,2,1,0:T(8,128)(2,1)S(1)}, bf16[4,8,2,32,128]{4,3,2,1,0:T(8,128)(2,1)S(1)}, bf16[1024,1024]{1,0:T(8,128)(2,1)S(1)}, bf16[1024...) custom-call(f32[2,8,1024]{2,1,0:T(8,128)S(1)} %get-tuple-element.20.bias_ref, ...), custom_call_target="tpu_custom_call" | custom-call | tf_op jit(solution)/shard_map/other_keys/pallas_call | solution.py:324
  32.6 0.2 collective-permute-start.1
  32.8 1.5 %rest.1 = (bf16[4,8,32,128]{3,2,1,0:T(8,128)(2,1)S(1)}, f32[4,8,2,32,128]{4,3,2,1,0:T(8,128)S(1)}) custom-call(bf16[4,1024,128]{2,1,0:T(8,128)(2,1)S(1)} %get-tuple-element.22.all_ref, bf16[1024,128]{1,0:T(8,128)(2,1)S(1)} %get-tuple-element.27.k_ref, f32[1024,1024]{1,0:T(8,128)S(1)} %get-tuple-element.28.e_ref, f32[1024,1024]{1,0:T(8,128)S(1)} %get-tuple-element.29.w_ref, ...), custom_call_target="tpu_custom_call" | custom-call | tf_op jit(solution)/shard_map/rest/pallas_call | solution.py:341
  34.3 0.3 collective-permute-done.1.recv_ref
  34.6 0.1 combine.1
  34.7 21.3 %all_to_all.11.x_ref = bf16[32,4,32,128]{3,2,1,0:T(8,128)(2,1)S(1)} all-to-all(bf16[32,4,32,128]{3,2,1,0:T(8,128)(2,1)S(1)} %bitcast.4), channel_id=1, replica_groups=mesh['cc'=8,'core'=2,'xh'=2,'y'=4] {'y','cc'}, dimensions={0} | all-to-all | bytes 2097152 | tf_op jit(solution)/shard_map/all_to_all | solution.py:358
  56.0 1.0 %unpack.1 = (bf16[32,4096]{1,0:T(8,128)(2,1)}, bf16[32,4096]{1,0:T(8,128)(2,1)}, bf16[32,4096]{1,0:T(8,128)(2,1)}, bf16[32,4096]{1,0:T(8,128)(2,1)}) custom-call(bf16[32,4,32,128]{3,2,1,0:T(8,128)(2,1)S(1)} %all_to_all.11.x_ref), custom_call_target="tpu_custom_call" | custom-call | tf_op jit(solution)/shard_map/unpack/pallas_call | solution.py:360
  (1 shorter events, 0.0 us)
Async XLA Ops:
  27.5 2.0 %collective-permute-start = (bf16[4,8,2,32,128]{4,3,2,1,0:T(8,128)(2,1)S(1)}, bf16[4,8,2,32,128]{4,3,2,1,0:T(8,128)(2,1)S(1)}, u32[]{:S(2)}, u32[]{:S(2)}) collective-permute-start(bf16[4,8,2,32,128]{4,3,2,1,0:T(8,128)(2,1)S(1)} %slice.4), channel_id=1, source_target_pairs={{0,8},{8,0},{1,9},{9,1},{2,10},{10,2},{3,11},{11,3},{4,12},{12,4},... | collective-permute-start | bytes 1572872 | tf_op jit(solution)/shard_map/ppermute | solution.py:307
  32.6 2.0 %collective-permute-start.1 = (bf16[4,8,2,32,128]{4,3,2,1,0:T(8,128)(2,1)S(1)}, bf16[4,8,2,32,128]{4,3,2,1,0:T(8,128)(2,1)S(1)}, u32[]{:S(2)}, u32[]{:S(2)}) collective-permute-start(bf16[4,8,2,32,128]{4,3,2,1,0:T(8,128)(2,1)S(1)} %get-tuple-element.35), channel_id=1, source_target_pairs={{0,8},{8,0},{1,9},{9,1},{2,10},{10,2},{3,11},{11,3},{4,12},{12,4},... | collective-permute-start | bytes 1572872 | tf_op jit(solution)/shard_map/ppermute | solution.py:340
